TPU v7x, 256 devices: a whole 4x4x8 slice. The times are simulated.
256 devices in a mesh: sta: 32 (over z, x), sat: 8 (over y, core).
Axes of the slice: x: 4, y: 4, z: 8, core: 2. Of those that a mesh axis runs over, the one named last changes fastest.
Arguments:
- sight: float32 [512, 3, 32, 256], P(('sta', 'sat')), may hold values from -1 to 1
- mapping: float32 [512, 32, 256], P(('sta', 'sat')), may hold values from 1 to 10
- residual: float32 [512, 32, 256], P(('sta', 'sat')), may hold values from -6 to 6
- counts: int32 [512, 32, 256], P(('sta', 'sat')), may hold values from 0 to 3, as said below
- track: int32 [512, 32], P(('sta', 'sat')), may hold values from 0 to 119, all different within a row
- knots: int32 [512, 256], P(('sta', 'sat')), may hold values from 0 to 3, as said below
- orbit: float32 [120, 3, 8, 256], P('sat'), may hold values from -6 to 6
Outputs:
- normal: float32 [960, 960], P('sat', 'sta')
- right_hand: float32 [960], P('sat')
- own_blocks: float32 [120, 8, 8], P('sat')
Inputs may be any that keep to these rules, and one draw needn't show every extreme that they name: `track`: each station's row names 32 different satellites, and every satellite is tracked by some station. `knots`: along the epochs of each station the index never falls, and every index from 0 to 3 occurs for every station. `counts`: some stations observe no satellite at all over a run of epochs.
All inputs are finite; a program needn't handle non-finite values.
Results may differ from a plain program's by a relative error of at most 0.00012.
Values sent between devices are 32-bit elements; how exact they have to be, the bound alone decides.
A program may use at most 256 MiB of HBM per device.

v0:
```python
import math

import jax
import jax.numpy as jnp
from jax import lax
from jax.sharding import PartitionSpec as P

KNOTS = 4


PRIOR = 1.0
HIGH = lax.Precision.HIGHEST


def reduce_station(
    station_sight, station_map, station_res, station_count, station_track, station_knot, orbit
):
    tracked = station_sight.shape[1]
    epochs = station_sight.shape[2]
    params = orbit.shape[2]
    span = tracked * params
    tracked_orbit = jnp.take(orbit, station_track, axis=0)
    design = jnp.sum(jnp.transpose(station_sight, (1, 0, 2))[:, :, None, :] * tracked_orbit, axis=1)
    weight = station_count.astype(jnp.float32)
    epoch_total = jnp.maximum(jnp.sum(weight, 0), 1.0)
    weighted = design * weight[:, None, :]
    weighted_rows = weighted.reshape(span, epochs)
    design_rows = design.reshape(span, epochs)
    clock_term = jnp.dot(weighted_rows / epoch_total, weighted_rows.T, precision=HIGH)
    slot_of = jnp.arange(span, dtype=jnp.int32) // params
    block_mask = (slot_of[:, None] == slot_of[None, :]).astype(jnp.float32)
    station_normal = jnp.dot(weighted_rows, design_rows.T, precision=HIGH) * block_mask - clock_term
    knot_select = (station_knot[None, :] == jnp.arange(KNOTS, dtype=jnp.int32)[:, None]).astype(
        jnp.float32
    )
    weight_map = weight * station_map
    sum_map = jnp.sum(weight_map, 0)
    sum_res = jnp.sum(weight * station_res, 0)
    tropo_rows = (weighted * station_map[:, None, :]).reshape(span, epochs) - weighted_rows * (
        sum_map / epoch_total
    )
    tropo_cross = jnp.dot(tropo_rows, knot_select.T, precision=HIGH)
    tropo_diag = (
        jnp.dot(
            knot_select,
            jnp.sum(weight_map * station_map, 0) - sum_map * sum_map / epoch_total,
            precision=HIGH,
        )
        + PRIOR
    )
    right_global = jnp.sum(
        (weighted * station_res[:, None, :]).reshape(span, epochs)
        - weighted_rows * (sum_res / epoch_total),
        1,
    )
    right_local = jnp.dot(
        knot_select,
        jnp.sum(weight_map * station_res, 0) - sum_map * sum_res / epoch_total,
        precision=HIGH,
    )
    scaled_cross = tropo_cross / tropo_diag
    station_normal = station_normal - jnp.dot(scaled_cross, tropo_cross.T, precision=HIGH)
    station_right = right_global - jnp.dot(scaled_cross, right_local, precision=HIGH)
    return (station_normal, station_right)


def spread_blocks(station_normal, station_right, station_track, sats, params):
    tracked = station_track.shape[0]
    span = tracked * params
    full_width = sats * params
    select = (station_track[:, None] == jnp.arange(sats, dtype=jnp.int32)[None, :]).astype(
        jnp.float32
    )
    rows_view = station_normal.reshape(tracked, params * span)
    left = jnp.dot(select.T, rows_view, precision=HIGH).reshape(full_width, span)
    left_turned = left.T.reshape(tracked, params * full_width)
    spread = jnp.dot(select.T, left_turned, precision=HIGH).reshape(full_width, full_width)
    right_spread = jnp.dot(
        select.T, station_right.reshape(tracked, params), precision=HIGH
    ).reshape(full_width)
    return (spread.T, right_spread)


def shards(sight, mapping, residual, counts, track, knots, orbit):
    all_orbit = lax.all_gather(orbit, "sat", axis=0, tiled=True)
    sats = all_orbit.shape[0]
    params = all_orbit.shape[2]
    full_width = sats * params

    def visit(station, carry):
        normal_sum, right_sum = carry
        station_normal, station_right = reduce_station(
            sight[station],
            mapping[station],
            residual[station],
            counts[station],
            track[station],
            knots[station],
            all_orbit,
        )
        spread, right_spread = spread_blocks(
            station_normal, station_right, track[station], sats, params
        )
        return (normal_sum + spread, right_sum + right_spread)

    start = (
        jnp.zeros((full_width, full_width), jnp.float32),
        jnp.zeros((full_width,), jnp.float32),
    )
    normal_sum, right_sum = lax.fori_loop(0, sight.shape[0], visit, start)
    stations = sight.shape[0] * lax.axis_size("sta") * lax.axis_size("sat")
    factor = sats / (stations * sight.shape[2] * sight.shape[3])
    cross_factor = sats / math.sqrt(stations * sight.shape[3])
    column_block = lax.psum_scatter(normal_sum, "sta", scatter_dimension=1, tiled=True)
    owned_block = lax.psum_scatter(column_block, "sat", scatter_dimension=0, tiled=True)
    diagonal_part = jnp.transpose(
        jnp.diagonal(normal_sum.reshape(sats, params, sats, params), axis1=0, axis2=2), (2, 0, 1)
    )
    right_all, blocks_all = lax.psum((right_sum, diagonal_part), ("sta", "sat"))
    own_sats = sats // lax.axis_size("sat")
    right_own = lax.dynamic_slice_in_dim(
        right_all, lax.axis_index("sat") * own_sats * params, own_sats * params
    )
    blocks_own = lax.dynamic_slice_in_dim(blocks_all, lax.axis_index("sat") * own_sats, own_sats)
    row_global = lax.axis_index("sat") * owned_block.shape[0] + jnp.arange(
        owned_block.shape[0], dtype=jnp.int32
    )
    column_global = lax.axis_index("sta") * owned_block.shape[1] + jnp.arange(
        owned_block.shape[1], dtype=jnp.int32
    )
    same_owner = row_global[:, None] // params == column_global[None, :] // params
    cross_part = jnp.where(same_owner, 0.0, owned_block)
    return (cross_part * cross_factor, right_own * factor, blocks_own * factor)


def solution(mesh):
    placed = (
        P(("sta", "sat"), None, None, None),
        P(("sta", "sat"), None, None),
        P(("sta", "sat"), None, None),
        P(("sta", "sat"), None, None),
        P(("sta", "sat"), None),
        P(("sta", "sat"), None),
        P("sat", None, None, None),
    )
    return jax.shard_map(
        shards,
        mesh=mesh,
        in_specs=placed,
        out_specs=(P("sat", "sta"), P("sat"), P("sat", None, None)),
        check_vma=False,
    )
```

profile of v0, /device:TPU:2, one launch (start us, length us, event | category | flops | bytes accessed | tf_op | source)
XLA Modules:
  0.0 439.6 jit_solution(10917095220936316313)
XLA Ops:
  7.2 0.7 all-gather.2.cloned.1.call-update
  8.0 34.2 %all-gather.2.cloned.1.call-done = f32[120,3,8,256]{3,2,1,0:T(8,128)} async-done(((f32[15,3,8,256]{3,2,1,0:T(8,128)}), f32[120,3,8,256]{3,2,1,0:T(8,128)}) %all-gather.2.cloned.1.call-update) | async-done | bytes 2949136 | tf_op jit(solution)/shard_map/all_gather | solution.py:85
  42.2 54.2 %while.18 = (s32[]{:T(128)}, f32[960,960]{0,1:T(8,128)}, f32[960]{0:T(1024)S(1)}, s32[2,32]{1,0:T(2,128)}, f32[2,3,32,256]{3,2,1,0:T(8,128)}, /*index=5*/f32[120...) while((s32[]{:T(128)}, f32[960,960]{0,1:T(8,128)}, ...), condition=%wide.region_8.9_spmd.clone, body=%wide.region_0.8_spmd.clone.sunk | while | flops 861211008 | bytes 36746156 | solution.py:110
  42.2 0.7 fusion.79
  42.9 2.4 gather_fusion
  45.4 0.9 dynamic-slice_bitcast_fusion.6
  46.3 0.7 compare_and_fusion.2
  47.2 0.8 multiply_reduce_fusion.8
  48.0 0.8 convert_reduce_fusion.2
  48.8 0.7 constant_dynamic-slice_fusion.4
  49.9 0.5 fusion.82
  50.4 0.4 convolution_select_fusion.2
  50.8 0.4 fusion.83
  51.3 0.7 fusion.84
  52.5 0.5 reshape.426
  53.0 3.6 fusion.85
  56.5 5.8 %reshape.427 = f32[960,960]{1,0:T(8,128)} reshape(f32[120,7680]{1,0:T(8,128)} %fusion.85) | data formatting | bytes 7372800 | tf_op jit(solution)/shard_map/while/body/eval_jaxpr/reshape | solution.py:77
  62.4 5.3 %bitcast_add_fusion.2 = f32[960,960]{0,1:T(8,128)} fusion(f32[960,960]{1,0:T(8,128)} %reshape.427, f32[960,960]{0,1:T(8,128)} %get-tuple-element.429, pred[]{:T(512)S(6)} %compare.27), kind=kLoop, calls=%fused_computation.2.clone.1 | loop fusion | flops 1843200 | bytes 11059201 | tf_op jit(solution)/shard_map/while/body/eval_jaxpr/add | solution.py:104
  68.8 0.7 fusion.79
  69.5 2.4 gather_fusion
  71.9 0.9 dynamic-slice_bitcast_fusion.6
  72.9 0.7 compare_and_fusion.2
  73.7 0.8 multiply_reduce_fusion.8
  74.5 0.8 convert_reduce_fusion.2
  75.3 0.7 constant_dynamic-slice_fusion.4
  76.4 0.5 fusion.82
  76.9 0.4 convolution_select_fusion.2
  77.4 0.4 fusion.83
  77.9 0.7 fusion.84
  79.0 0.5 reshape.426
  79.5 3.6 fusion.85
  83.1 5.8 %reshape.427 = f32[960,960]{1,0:T(8,128)} reshape(f32[120,7680]{1,0:T(8,128)} %fusion.85) | data formatting | bytes 7372800 | tf_op jit(solution)/shard_map/while/body/eval_jaxpr/reshape | solution.py:77
  88.9 6.5 %bitcast_add_fusion.2 = f32[960,960]{0,1:T(8,128)} fusion(f32[960,960]{1,0:T(8,128)} %reshape.427, f32[960,960]{0,1:T(8,128)} %get-tuple-element.429, pred[]{:T(512)S(6)} %compare.27), kind=kLoop, calls=%fused_computation.2.clone.1 | loop fusion | flops 1843200 | bytes 11059201 | tf_op jit(solution)/shard_map/while/body/eval_jaxpr/add | solution.py:104
  96.5 88.8 %fusion = f32[960,32]{0,1:T(8,128)S(1)} fusion(f32[960,960]{0,1:T(8,128)} %get-tuple-element.247), kind=kCustom, calls=%all-reduce-scatter | all-reduce-scatter fusion | flops 983041 | bytes 3810304
  185.4 3.4 collective-permute-start
  188.8 0.6 dynamic-slice.6
  190.0 0.6 dynamic-slice.2
  191.3 2.5 collective-permute-start.1
  193.8 31.4 %reshape.409 = f32[120,8,120,8]{1,0,3,2:T(8,128)} reshape(f32[960,960]{0,1:T(8,128)} %get-tuple-element.247) | data formatting | bytes 7372800 | tf_op jit(solution)/shard_map/reshape | solution.py:117
  225.3 58.8 %copy.26 = f32[120,8,120,8]{3,1,2,0:T(8,128)} copy(f32[120,8,120,8]{1,0,3,2:T(8,128)} %reshape.409) | data formatting | bytes 7372800 | tf_op jit(solution)/shard_map/reshape | solution.py:117
  284.1 2.3 gather_fusion.1
  286.3 79.2 %all-reduce.3 = (f32[960]{0:T(1024)S(1)}, f32[120,8,8]{2,1,0:T(8,128)S(1)}) all-reduce(f32[960]{0:T(1024)S(1)} %get-tuple-element.248, f32[120,8,8]{2,1,0:T(8,128)S(1)} %gather_fusion.1), channel_id=1, replica_groups=mesh['sta'=32,'sat'=8] {'sta','sat'}, use_global_device_ids=true, to_apply=%region_11.12 | all-reduce | flops 8640 | bytes 69120 | tf_op jit(solution)/shard_map/psum | solution.py:119
  365.5 0.7 copy.27
  366.3 0.4 concatenate.7
  366.6 0.7 constant_dynamic-slice_fusion.2
  367.3 0.6 dynamic-slice_multiply_fusion.1
  367.9 63.4 %all-reduce.6.cloned.1.call-done = f32[960,30]{0,1:T(8,128)} async-done(((f32[960,30]{0,1:T(8,128)}), f32[960,30]{0,1:T(8,128)}) %all-reduce.6.cloned.1.call-update) | async-done | bytes 115216
  431.4 1.4 fusion.36
  (54 shorter events, 4.7 us)
Async XLA Ops:
  7.2 35.1 %all-gather.2.cloned.1.call-start = ((), (), s32[]{:S(2)}) async-start(), calls=%async_computation | async-start | bytes 3317760 | tf_op jit(solution)/shard_map/all_gather | solution.py:85
  7.9 423.5 %all-reduce.6.cloned.1.call-start = ((), (), s32[]{:S(2)}) async-start(), calls=%async_computation.1 | async-start | bytes 262144
  96.5 92.3 %copy-start = (u32[256]{0:T(256)S(1)}, u32[256]{0:T(256)}, u32[]{:S(2)}) copy-start(u32[256]{0:T(256)} %constant.208) | copy-start | bytes 3076
  96.5 93.5 %copy-start.1 = (u32[256]{0:T(256)S(1)}, u32[256]{0:T(256)}, u32[]{:S(2)}) copy-start(u32[256]{0:T(256)} %constant.212) | copy-start | bytes 3076
  185.4 180.9 %collective-permute-start = (f32[960,32]{0,1:T(8,128)S(1)}, f32[960,32]{0,1:T(8,128)S(1)}, u32[]{:S(2)}, u32[]{:S(2)}) collective-permute-start(f32[960,32]{0,1:T(8,128)S(1)} %fusion), channel_id=1, source_target_pairs={{0,8},{8,16},{16,24},{24,32},{32,40},{40,48},{48,56},{56,64},{64,7... | collective-permute-start | bytes 368648
  191.3 175.0 %collective-permute-start.1 = (f32[960,30]{0,1:T(8,128)S(1)}, f32[960,30]{0,1:T(8,128)S(1)}, u32[]{:S(2)}, u32[]{:S(2)}) collective-permute-start(f32[960,30]{0,1:T(8,128)S(1)} %slice.4), channel_id=1, source_target_pairs={{0,16},{8,24},{16,32},{24,40},{32,48},{40,56},{48,64},{56,72},{64,... | collective-permute-start | bytes 345608
Sparse Core Ops, SparseCore 0:
  9.8 32.3 all-gather.1
  367.5 63.8 all-reduce.5
where the time goes:
time: 443 us; the launch traced here: 440 us
  blocking collectives  168 us (38%)
  local copies, waits for them, and re-layouts  118 us (27%)
  waiting for transfers between devices  98.4 us (22%)
  other arithmetic  20.4 us (5%)
  between operations  15.5 us (3%)
  matrix products  13.2 us (3%)
  starting transfers between devices  5.97 us (1%)
    reshape x2, local copies, waits for them, and re-layouts, shards(): normal_sum.reshape(sats, params, sats, params)  90.3 us
    unnamed x1, blocking collectives  88.8 us
    psum x1, blocking collectives, shards(): right_all, blocks_all = lax.psum((right_sum, diagonal_part), ('sta', 'sat'))  79.2 us
    unnamed x5, waiting for transfers between devices  64.1 us
    all_gather x1, waiting for transfers between devices, shards(): all_orbit = lax.all_gather(orbit, 'sat', axis=0, tiled=True)  34.2 us
    add x4, other arithmetic, visit(): return (normal_sum + spread, right_sum + right_spread)  11.8 us
    reshape x2, local copies, waits for them, and re-layouts, spread_blocks(): jnp.dot(select.T, left_turned, precision=HIGH)  11.7 us
  transfers between devices with their start and end apart: 4, of which 2 were waited for; matrix products, arithmetic and copies ran while one was open for 22% of the time, Pallas kernels for 0%

commit v1 on v0

v1 whole, which is shorter than its diff:
```python
import functools
import math

import jax
import jax.numpy as jnp
from jax import lax
from jax.experimental import pallas as pl
from jax.experimental.pallas import tpu as pltpu
from jax.sharding import PartitionSpec as P

F32 = jnp.float32
BF16 = jnp.bfloat16
MESH = pl.DeviceIdType.MESH
HIGH = lax.Precision.HIGHEST

SATS = 120
OWN = 15
PAR = 8
SLOTS = 32
EPOCHS = 256
KNOTS = 4
PRIOR = 1.0
NY = 4
NX = 4
NZ = 8
ROWS = 120
COVER = 40
CUT = 8
ZA = 5
ANY = pl.BlockSpec(memory_space=pl.ANY)
VMEM = pl.BlockSpec(memory_space=pltpu.VMEM)
SMEM = pl.BlockSpec(memory_space=pltpu.SMEM)


def place():
    sta = lax.axis_index("sta")
    sat = lax.axis_index("sat")
    return sta // NX, sta % NX, sat // 2, sat % 2


def remote(src, dst, send, recv, device):
    return pltpu.make_async_remote_copy(
        src_ref=src,
        dst_ref=dst,
        send_sem=send,
        recv_sem=recv,
        device_id=device,
        device_id_type=MESH,
    )


def greet(peers):
    barrier = pltpu.get_barrier_semaphore()
    for peer in peers:
        pl.semaphore_signal(barrier, inc=1, device_id=peer, device_id_type=MESH)
    pl.semaphore_wait(barrier, len(peers))


def gather_kernel(*refs):
    orbit = refs[0]
    stations = refs[1:7]
    full = refs[7]
    others = refs[8:14]
    send, recv, local = refs[14:]
    z, x, y, c = place()
    sta = z * NX + x
    right = (sta, ((y + 1) % NY) * 2 + c)
    left = (sta, ((y + NY - 1) % NY) * 2 + c)
    mate = (sta, y * 2 + 1 - c)
    greet((right, left, mate))

    mine = (y * 2 + c) * OWN
    from_left = (((y + NY - 1) % NY) * 2 + c) * OWN
    from_right = (((y + 1) % NY) * 2 + c) * OWN
    from_far = (((y + 2) % NY) * 2 + c) * OWN
    head, tail = (0, CUT), (CUT, OWN - CUT)

    def part(base, cut):
        return full.at[pl.ds(base + cut[0], cut[1])]

    def own(cut):
        return orbit.at[pl.ds(cut[0], cut[1])]

    def go(slot, src, dst, device):
        copy = remote(src, dst, send.at[slot], recv.at[slot], device)
        copy.start()
        return copy

    copies = []
    right_head = go(0, own(head), part(mine, head), right)
    left_tail = go(1, own(tail), part(mine, tail), left)
    right_tail = go(2, own(tail), part(mine, tail), right)
    left_head = go(3, own(head), part(mine, head), left)
    keep = pltpu.make_async_copy(orbit, full.at[pl.ds(mine, OWN)], local)
    keep.start()
    mates = [go(6 + i, a, b, mate) for i, (a, b) in enumerate(zip(stations, others))]
    mates.append(go(12, orbit, full.at[pl.ds(mine, OWN)], mate))

    right_head.wait_recv()
    relay_right = go(4, part(from_left, head), part(from_left, head), right)
    mates.append(go(13, part(from_left, head), part(from_left, head), mate))
    left_tail.wait_recv()
    relay_left = go(5, part(from_right, tail), part(from_right, tail), left)
    mates.append(go(14, part(from_right, tail), part(from_right, tail), mate))
    right_tail.wait_recv()
    mates.append(go(15, part(from_left, tail), part(from_left, tail), mate))
    left_head.wait_recv()
    mates.append(go(16, part(from_right, head), part(from_right, head), mate))
    relay_right.wait_recv()
    mates.append(go(17, part(from_far, head), part(from_far, head), mate))
    relay_left.wait_recv()
    mates.append(go(18, part(from_far, tail), part(from_far, tail), mate))
    for copy in mates:
        copy.wait_recv()
    for copy in (right_head, left_tail, right_tail, left_head, relay_right, relay_left):
        copy.wait_send()
    for copy in mates:
        copy.wait_send()
    keep.wait()


def halves(value):
    high = value.astype(BF16)
    low = (value - high.astype(F32)).astype(BF16)
    return high, low


def turned(a, b, precision=None):
    return lax.dot_general(
        a, b, (((1,), (1,)), ((), ())), preferred_element_type=F32, precision=precision
    )


def product(a_high, a_low, b_high, b_low):
    return turned(a_high, b_high) + turned(a_high, b_low) + turned(a_low, b_high)


def tile_of(sat):
    group = sat // OWN
    return ((group % 2) * 4 + group // 2) * 16 + sat % OWN


def station_kernel(
    track_a, track_b, orbit, *refs
):
    mine = refs[0:5]
    other = refs[5:10]
    normal, small = refs[10:12]
    (factor, diagonal, extra, rows_w, rows_t, rows_r, rows_d, sides, f_high, f_low,
     r_high, r_low, e_high, e_low) = refs[12:]
    core = lax.axis_index("sat") % 2

    factor[...] = jnp.zeros_like(factor)
    diagonal[...] = jnp.zeros_like(diagonal)
    extra[...] = jnp.zeros_like(extra)
    local_rows = jnp.zeros((8, 128), F32)

    for index in range(4):
        sight, mapping, residual, counts, knots = mine if index < 2 else other
        track = track_a if index < 2 else track_b
        s = index % 2
        weight = counts[s].astype(F32)
        path = mapping[s]
        seen = residual[s]
        total = jnp.maximum(jnp.sum(weight, 0, keepdims=True), 1.0)
        share = 1.0 / total
        weight_map = weight * path
        sum_map = jnp.sum(weight_map, 0, keepdims=True)
        sum_res = jnp.sum(weight * seen, 0, keepdims=True)
        rows_w[...] = weight * lax.rsqrt(total)
        rows_t[...] = weight * (path - sum_map * share)
        rows_r[...] = weight * (seen - sum_res * share)
        rows_d[...] = jnp.sqrt(weight)
        square = jnp.sum(weight_map * path, 0, keepdims=True) - sum_map * sum_map * share
        cross = jnp.sum(weight_map * seen, 0, keepdims=True) - sum_map * sum_res * share
        lane_rows = lax.broadcasted_iota(jnp.int32, (128, EPOCHS), 0)
        pick = lane_rows == knots[s : s + 1, :] + KNOTS * index
        knot_rows = jnp.where(pick, 1.0, 0.0)
        last_rows = jnp.where(lane_rows == 16, 1.0, 0.0)
        row8 = lax.broadcasted_iota(jnp.int32, (8, EPOCHS), 0)
        pair = jnp.where(row8 == 0, square, jnp.where(row8 == 1, cross, 0.0))
        local_rows = local_rows + turned(pair, knot_rows, HIGH)
        lanes = slice(index * EPOCHS, (index + 1) * EPOCHS)

        def visit(m, carry):
            sat = track[s, m]
            tile = tile_of(sat)
            design = (
                sight[s, 0, pl.ds(m, 1), :] * orbit[sat, 0]
                + sight[s, 1, pl.ds(m, 1), :] * orbit[sat, 1]
                + sight[s, 2, pl.ds(m, 1), :] * orbit[sat, 2]
            )
            factor[tile, :, lanes] = design * rows_w[pl.ds(m, 1), :]
            diagonal[tile, :, lanes] = design * rows_d[pl.ds(m, 1), :]
            sides[m, :, 0:EPOCHS] = design * rows_t[pl.ds(m, 1), :]
            sides[m, :, EPOCHS : 2 * EPOCHS] = design * rows_r[pl.ds(m, 1), :]
            return carry

        lax.fori_loop(0, SLOTS, visit, 0, unroll=4)
        high, low = halves(sides[...].reshape(SLOTS * PAR, 2 * EPOCHS))
        pickers = jnp.concatenate([knot_rows, last_rows], axis=1).astype(BF16)
        crossed = (turned(high, pickers) + turned(low, pickers)).reshape(SLOTS, PAR, 128)
        sides[:, :, 0:128] = crossed

        def spread(m, carry):
            tile = tile_of(track[s, m])
            extra[tile] = extra[tile] + sides[m, :, 0:128]
            return carry

        lax.fori_loop(0, SLOTS, spread, 0, unroll=4)

    lane = lax.broadcasted_iota(jnp.int32, (1, 128), 1)
    scale = jnp.where(lane < 16, lax.rsqrt(local_rows[0:1] + PRIOR), 0.0)
    special = jnp.where(lane == 16, -1.0, local_rows[1:2] * scale)
    row = lax.broadcasted_iota(jnp.int32, (8, 128), 0)
    extra[15] = jnp.where(row == 0, special, 0.0)
    first = core * 64

    for block in range(8):
        rows = slice(block * 128, (block + 1) * 128)
        tiles = slice(block * 16, (block + 1) * 16)
        high, low = halves(factor[tiles].reshape(128, 4 * EPOCHS))
        f_high[rows, 0 : 4 * EPOCHS] = high
        f_low[rows, 0 : 4 * EPOCHS] = low
        side = extra[tiles].reshape(128, 128)
        if block == 0:
            special_row = lax.broadcasted_iota(jnp.int32, (128, 128), 0) >= ROWS
            side = jnp.where(special_row, side, side * scale)
        else:
            side = side * scale
        high, low = halves(side)
        f_high[rows, 4 * EPOCHS :] = high
        f_low[rows, 4 * EPOCHS :] = low

    tail = jnp.where(lane < 16, scale, 1.0)
    for block in range(4):
        rows = slice(block * 128, (block + 1) * 128)
        source = pl.ds(pl.multiple_of(core * 512, 512) + block * 128, 128)
        r_high[rows, 0 : 4 * EPOCHS] = f_high[source, 0 : 4 * EPOCHS]
        r_low[rows, 0 : 4 * EPOCHS] = f_low[source, 0 : 4 * EPOCHS]
        side = extra[pl.ds(first + block * 16, 16)].reshape(128, 128) * tail
        high, low = halves(side)
        r_high[rows, 4 * EPOCHS :] = high
        r_low[rows, 4 * EPOCHS :] = low

    for block in range(8):
        rows = slice(block * 128, (block + 1) * 128)
        result = product(f_high[rows], f_low[rows], r_high[...], r_low[...])
        group = (block % 4) * 2 + block // 4
        for slab in range(NY):
            normal[slab, group] = -result[:, slab * 128 : (slab + 1) * 128]

    own_row = lax.broadcasted_iota(jnp.int32, (128, 128), 0) // PAR
    own_lane = lax.broadcasted_iota(jnp.int32, (128, 128), 1) // PAR
    for slab in range(NY):
        high, low = halves(diagonal[pl.ds(first + slab * 16, 16)].reshape(128, 4 * EPOCHS))
        block = product(high, low, high, low) + normal[slab, slab * 2 + core]
        block = jnp.where(own_row == own_lane, block, 0.0).reshape(16, PAR, 128)
        small[slab, 0:8] = jnp.sum(block, 0)
        small[slab, 8:16] = normal[slab, 0, ROWS : ROWS + 8, :]


def ring_start(view, me, buffers, sems, device):
    far, right, left = (me + 2) % 4, (me + 1) % 4, (me + 3) % 4
    b_0, b_1, l_0, l_1, r_0, r_1 = buffers[:6]
    send, recv = sems
    plan = (
        (view(far, 0), b_0, right),
        (view(far, 1), b_1, left),
        (view(right, 1), l_1, right),
        (view(left, 0), r_0, left),
    )
    copies = []
    for slot, (src, dst, peer) in enumerate(plan):
        copy = remote(src, dst, send.at[slot], recv.at[slot], device(peer))
        copy.start()
        copies.append(copy)
    return copies


def ring_middle(view, me, buffers, sems, device, copies):
    right, left = (me + 1) % 4, (me + 3) % 4
    b_0, b_1, l_0, l_1, r_0, r_1, s_0, s_1 = buffers
    send, recv = sems
    copies[0].wait_recv()
    s_0[...] = view(right, 0)[...] + b_0[...]
    one = remote(s_0, l_0, send.at[4], recv.at[4], device(right))
    one.start()
    copies[1].wait_recv()
    s_1[...] = view(left, 1)[...] + b_1[...]
    two = remote(s_1, r_1, send.at[5], recv.at[5], device(left))
    two.start()
    return copies + [one, two]


def ring_finish(view, me, buffers, copies, out_0, out_1):
    b_0, b_1, l_0, l_1, r_0, r_1 = buffers[:6]
    for index in (2, 3, 4, 5):
        copies[index].wait_recv()
    out_0[...] = view(me, 0)[...] + l_0[...] + r_0[...]
    out_1[...] = view(me, 1)[...] + l_1[...] + r_1[...]


def reduce_kernel(normal, small, out, out_small, *refs):
    bufs = [refs[i * 8 : (i + 1) * 8] for i in range(4)]
    (y_part, x_part, total, arrived, small_y, small_x, small_z, hold_x, hold_z) = refs[32:41]
    sems = [(refs[41 + 2 * i], refs[42 + 2 * i]) for i in range(4)]
    z_send, z_recv, s_send, s_recv = refs[49:]
    z, x, y, c = place()

    def at_y(peer):
        return (z * NX + x, peer * 2 + c)

    def at_x(peer):
        return (z * NX + peer, y * 2 + c)

    def at_z(peer):
        return (peer * NX + x, y * 2 + c)

    greet(
        [at_y((y + k) % NY) for k in range(1, NY)]
        + [at_x((x + k) % NX) for k in range(1, NX)]
        + [at_z((z + k) % NZ) for k in range(1, NZ)]
    )

    def rows_of(peer):
        return pl.ds(pl.multiple_of(jnp.minimum(peer * 30 // 8, 10) * 8, 8), COVER)

    a_cut = (pl.ds(0, 3), pl.ds(3, ZA - 3))
    b_cut = (pl.ds(0, 2), pl.ds(2, 1))

    def ay_view(peer, half):
        return normal.at[peer, a_cut[half], pl.ds(0, ROWS)]

    def bx_view(peer, half):
        return normal.at[pl.ds(2 * half, 2), pl.ds(ZA, NZ - ZA), rows_of(peer)]

    def ax_view(peer, half):
        return y_part.at[a_cut[half], rows_of(peer)]

    def by_view(peer, half):
        return x_part.at[peer, b_cut[half]]

    def small_start(base, source, target, me, size, device):
        copies = []
        for k in range(1, size):
            peer = (me + k) % size
            slot = base + k - 1
            copy = remote(
                source(peer), target.at[me], s_send.at[slot], s_recv.at[slot], device(peer)
            )
            copy.start()
            copies.append(copy)
        return copies

    def small_sum(copies, target, me, own, size):
        target[me] = own
        for copy in copies:
            copy.wait_recv()
        result = target[0]
        for k in range(1, size):
            result = result + target[k]
        return result

    sy = small_start(0, lambda peer: small.at[peer], small_y, y, NY, at_y)
    ay = ring_start(ay_view, y, bufs[0], sems[0], at_y)
    bx = ring_start(bx_view, x, bufs[1], sems[1], at_x)
    ay = ring_middle(ay_view, y, bufs[0], sems[0], at_y, ay)
    bx = ring_middle(bx_view, x, bufs[1], sems[1], at_x, bx)

    hold_x[...] = small_sum(sy, small_y, y, small[y], NY)
    sx = small_start(3, lambda peer: hold_x, small_x, x, NX, at_x)

    ring_finish(ay_view, y, bufs[0], ay, y_part.at[a_cut[0]], y_part.at[a_cut[1]])
    ax = ring_start(ax_view, x, bufs[2], sems[2], at_x)
    ring_finish(
        bx_view, x, bufs[1], bx, x_part.at[pl.ds(0, 2)], x_part.at[pl.ds(2, 2)]
    )
    by = ring_start(by_view, y, bufs[3], sems[3], at_y)

    hold_z[...] = small_sum(sx, small_x, x, hold_x[...], NX)
    sz = small_start(6, lambda peer: hold_z, small_z, z, NZ, at_z)

    ax = ring_middle(ax_view, x, bufs[2], sems[2], at_x, ax)
    by = ring_middle(by_view, y, bufs[3], sems[3], at_y, by)
    ring_finish(ax_view, x, bufs[2], ax, total.at[pl.ds(0, 3)], total.at[pl.ds(3, ZA - 3)])
    ring_finish(by_view, y, bufs[3], by, total.at[pl.ds(ZA, 2)], total.at[pl.ds(ZA + 2, 1)])

    last = []
    for k in (4, 3, 5, 2, 6, 1, 7):
        peer = (z + k) % NZ
        copy = remote(
            total.at[peer], arrived.at[k - 1], z_send.at[k - 1], z_recv.at[k - 1], at_z(peer)
        )
        copy.start()
        last.append((k, copy))
    out_small[...] = small_sum(sz, small_z, z, hold_z[...], NZ)
    value = total[z]
    for k, copy in reversed(last):
        copy.wait_recv()
        value = value + arrived[k - 1]
    out[...] = value
    for copies in (sy, sx, sz, ay, bx, ax, by):
        for copy in copies:
            copy.wait_send()
    for k, copy in last:
        copy.wait_send()


def ring_buffers(half_0, half_1):
    shapes = [half_0, half_1, half_0, half_1, half_0, half_1, half_0, half_1]
    return [pltpu.VMEM(shape, F32) for shape in shapes]


def shards(sight, mapping, residual, counts, track, knots, orbit):
    shape = jax.ShapeDtypeStruct
    stations = (sight, mapping, residual, counts, track, knots)
    gathered = pl.pallas_call(
        gather_kernel,
        name="gather",
        out_shape=[shape((SATS, 3, PAR, EPOCHS), F32)]
        + [shape(a.shape, a.dtype) for a in stations],
        in_specs=[ANY] * 7,
        out_specs=[ANY] * 7,
        scratch_shapes=[
            pltpu.SemaphoreType.DMA((19,)),
            pltpu.SemaphoreType.DMA((19,)),
            pltpu.SemaphoreType.DMA,
        ],
        compiler_params=pltpu.CompilerParams(collective_id=0, has_side_effects=True),
    )(orbit, *stations)
    full, sight_b, mapping_b, residual_b, counts_b, track_b, knots_b = gathered

    big = 4 * EPOCHS
    wide = big + 128
    normal, small = pl.pallas_call(
        station_kernel,
        name="stations",
        out_shape=[shape((NY, NZ, 128, 128), F32), shape((NY, 16, 128), F32)],
        in_specs=[SMEM, SMEM] + [VMEM] * 11,
        out_specs=[VMEM, VMEM],
        scratch_shapes=[
            pltpu.VMEM((128, PAR, big), F32),
            pltpu.VMEM((128, PAR, big), F32),
            pltpu.VMEM((128, PAR, 128), F32),
            pltpu.VMEM((SLOTS, EPOCHS), F32),
            pltpu.VMEM((SLOTS, EPOCHS), F32),
            pltpu.VMEM((SLOTS, EPOCHS), F32),
            pltpu.VMEM((SLOTS, EPOCHS), F32),
            pltpu.VMEM((SLOTS, PAR, 2 * EPOCHS), F32),
            pltpu.VMEM((1024, wide), BF16),
            pltpu.VMEM((1024, wide), BF16),
            pltpu.VMEM((512, wide), BF16),
            pltpu.VMEM((512, wide), BF16),
            pltpu.VMEM((8, 128), BF16),
            pltpu.VMEM((8, 128), BF16),
        ],
        compiler_params=pltpu.CompilerParams(vmem_limit_bytes=60 * 1024 * 1024),
    )(
        track, track_b, full, sight, mapping, residual, counts, knots,
        sight_b, mapping_b, residual_b, counts_b, knots_b,
    )

    nb = NZ - ZA
    scratch = (
        ring_buffers((3, ROWS, 128), (ZA - 3, ROWS, 128))
        + ring_buffers((2, nb, COVER, 128), (2, nb, COVER, 128))
        + ring_buffers((3, COVER, 128), (ZA - 3, COVER, 128))
        + ring_buffers((2, COVER, 128), (1, COVER, 128))
        + [
            pltpu.VMEM((ZA, ROWS, 128), F32),
            pltpu.VMEM((NY, nb, COVER, 128), F32),
            pltpu.VMEM((NZ, COVER, 128), F32),
            pltpu.VMEM((NZ - 1, COVER, 128), F32),
            pltpu.VMEM((NY, 16, 128), F32),
            pltpu.VMEM((NX, 16, 128), F32),
            pltpu.VMEM((NZ, 16, 128), F32),
            pltpu.VMEM((16, 128), F32),
            pltpu.VMEM((16, 128), F32),
        ]
        + [pltpu.SemaphoreType.DMA((6,))] * 8
        + [
            pltpu.SemaphoreType.DMA((7,)),
            pltpu.SemaphoreType.DMA((7,)),
            pltpu.SemaphoreType.DMA((13,)),
            pltpu.SemaphoreType.DMA((13,)),
        ]
    )
    block, sums = pl.pallas_call(
        reduce_kernel,
        name="reduce",
        out_shape=[shape((COVER, 128), F32), shape((16, 128), F32)],
        in_specs=[VMEM, VMEM],
        out_specs=[VMEM, VMEM],
        scratch_shapes=scratch,
        compiler_params=pltpu.CompilerParams(collective_id=1, has_side_effects=True),
    )(normal, small)

    z, x, y, c = place()
    skip = x * 30 - jnp.minimum(x * 30 // 8, 10) * 8
    cross_factor = SATS / math.sqrt(512 * EPOCHS)
    factor = SATS / (512 * SLOTS * EPOCHS)
    owned = lax.dynamic_slice(block, (skip, 0), (30, ROWS)).T
    row = (y * 2 + c) * OWN + jnp.arange(ROWS, dtype=jnp.int32)[:, None] // PAR
    column = ((z * NX + x) * 30 + jnp.arange(30, dtype=jnp.int32)[None, :]) // PAR
    cross_part = jnp.where(row == column, 0.0, owned) * cross_factor
    right = sums[8, :ROWS] * factor
    blocks = jnp.transpose(sums[0:8, :ROWS].reshape(PAR, OWN, PAR), (1, 0, 2)) * factor
    return cross_part, right, blocks


def solution(mesh):
    placed = (
        P(("sta", "sat"), None, None, None),
        P(("sta", "sat"), None, None),
        P(("sta", "sat"), None, None),
        P(("sta", "sat"), None, None),
        P(("sta", "sat"), None),
        P(("sta", "sat"), None),
        P("sat", None, None, None),
    )
    return jax.shard_map(
        shards,
        mesh=mesh,
        in_specs=placed,
        out_specs=(P("sat", "sta"), P("sat"), P("sat", None, None)),
        check_vma=False,
    )
```

time: 443 us -> 80.5 us (0.18)
  blocking collectives: 168 us -> 0 us
  local copies, waits for them, and re-layouts: 118 us -> 0.82 us
  waiting for transfers between devices: 98.4 us -> 0 us
  Pallas kernels: 0 us -> 75.3 us
  other arithmetic: 20.4 us -> 3.31 us
  between operations: 15.5 us -> 0.75 us
  matrix products: 13.2 us -> 0 us
  starting transfers between devices: 5.97 us -> 0 us
    reshape x16 -> x0, local copies, waits for them, and re-layouts: 104 us -> none  [the longest x2 90.3 us: shards(): normal_sum.reshape(sats, params, sats, params)]
    unnamed x1 -> x0, blocking collectives: 88.8 us -> none
    psum x1 -> x0, blocking collectives: 79.2 us -> none  [shards(): right_all, blocks_all = lax.psum((right_sum, diagonal_part), ('sta', 'sat'))]
    pallas_call x0 -> x3, Pallas kernels: none -> 75.3 us  [the longest x1 35.9 us: shards(): pl.pallas_call(reduce_kernel, name='reduce', out_shape=[shape((COVER, 128...]
    unnamed x5 -> x0, waiting for transfers between devices: 64.1 us -> none
    all_gather x1 -> x0, waiting for transfers between devices: 34.2 us -> none  [shards(): all_orbit = lax.all_gather(orbit, 'sat', axis=0, tiled=True)]
    dot_general x20 -> x0, matrix products: 13.2 us -> none  [the longest x2 7.11 us: spread_blocks(): jnp.dot(select.T, left_turned, precision=HIGH)]
    add x4 -> x1, other arithmetic: 11.8 us -> 0.01 us  [shards(): row = (y * 2 + c) * OWN + jnp.arange(ROWS, dtype=jnp.int32)[:, None] // PAR]
  transfers between devices with their start and end apart: 4 -> 0, of which waited for: 2 -> 0; matrix products, arithmetic and copies ran while one was open for 22% -> 0% of each run, Pallas kernels for 0% -> 0%
where the time goes in v1:
time: 80.5 us; the launch traced here: 80.2 us
  Pallas kernels  75.3 us (94%)
  other arithmetic  3.31 us (4%)
  local copies, waits for them, and re-layouts  0.82 us (1%)
    pallas_call x1, Pallas kernels, shards(): pl.pallas_call(reduce_kernel, name='reduce', out_shape=[shape((COVER, 128...  35.9 us
    pallas_call x1, Pallas kernels, shards(): pl.pallas_call(station_kernel, name='stations', out_shape=[shape((NY, NZ,...  20.5 us
    pallas_call x1, Pallas kernels, shards(): pl.pallas_call(gather_kernel, name='gather', out_shape=[shape((SATS, 3, P...  19 us

profile of v1, /device:TPU:2, one launch (start us, length us, event | category | flops | bytes accessed | tf_op | source)
XLA Modules:
  0.0 80.2 jit_solution(6105428518152523810)
XLA Ops:
  0.6 19.0 %gather.1 = (f32[120,3,8,256]{3,2,1,0:T(8,128)}, f32[2,3,32,256]{3,2,1,0:T(8,128)}, f32[2,32,256]{2,1,0:T(8,128)}, f32[2,32,256]{2,1,0:T(8,128)}, s32[2,32,256]{...) custom-call(f32[15,3,8,256]{3,2,1,0:T(8,128)} %refs_0_.2, f32[2,3,32,256]{3,2,1,0:T(8,128)} %refs_0_.3, ...), custom_call_target="tpu_custom_call" | custom-call | tf_op jit(solution)/shard_map/gather/pallas_call | solution.py:418
  19.6 20.5 %stations.1 = (f32[4,8,128,128]{3,2,1,0:T(8,128)}, f32[4,16,128]{2,1,0:T(8,128)}) custom-call(s32[2,32]{1,0:T(2,128)} %track_a.1, s32[2,32]{1,0:T(2,128)} %get-tuple-element.14.track_b, f32[120,3,8,256]{3,2,1,0:T(8,128)} %get-tuple-element.15.orbit, f32[2,3,32,256]{3,2,1,0:T(8,128)} %refs_0_.3, f32[2,32,256]{2,1,0:T(8,128)} %refs_1_.3, ...), custom_call_target="tpu_custom_call" | custom-call | tf_op jit(solution)/shard_map/stations/pallas_call | solution.py:436
  40.1 35.9 %reduce.1 = (f32[40,128]{1,0:T(8,128)}, f32[16,128]{1,0:T(8,128)}) custom-call(f32[4,8,128,128]{3,2,1,0:T(8,128)} %get-tuple-element.21.normal, f32[4,16,128]{2,1,0:T(8,128)} %get-tuple-element.22.small), custom_call_target="tpu_custom_call" | custom-call | tf_op jit(solution)/shard_map/reduce/pallas_call | solution.py:489
  76.1 1.4 %fusion = f32[120,30]{0,1:T(8,128)} fusion(f32[40,128]{1,0:T(8,128)} %get-tuple-element.23, s32[]{:T(128)S(6)} %select_n.55, s32[120]{0:T(128)S(1)} %fusion.1, s32[30]{0:T(128)S(1)} %and_select_fusion), kind=kLoop, calls=%fused_computation.1 | loop fusion | flops 10800 | bytes 29404 | tf_op jit(solution)/shard_map/mul | solution.py:506
  77.5 1.2 %multiply_bitcast_fusion = f32[120]{0:T(128)} fusion(f32[16,128]{1,0:T(8,128)} %get-tuple-element.24), kind=kLoop, calls=%fused_computation.12 | loop fusion | flops 120 | bytes 960 | tf_op jit(solution)/shard_map/mul | solution.py:507
  78.7 0.7 slice_multiply_fusion
  79.4 0.1 mul.59
  79.5 0.7 copy.11
  (2 shorter events, 0.0 us)

commit v2 on v1

v2 whole, which is shorter than its diff:
```python
import functools
import math

import jax
import jax.numpy as jnp
from jax import lax
from jax.experimental import pallas as pl
from jax.experimental.pallas import tpu as pltpu
from jax.sharding import PartitionSpec as P

F32 = jnp.float32
BF16 = jnp.bfloat16
MESH = pl.DeviceIdType.MESH
HIGH = lax.Precision.HIGHEST

SATS = 120
OWN = 15
PAR = 8
SLOTS = 32
EPOCHS = 256
KNOTS = 4
PRIOR = 1.0
NY = 4
NX = 4
NZ = 8
ROWS = 120
COVER = 40
CUT = 8
ZA = 5
ANY = pl.BlockSpec(memory_space=pl.ANY)
VMEM = pl.BlockSpec(memory_space=pltpu.VMEM)
SMEM = pl.BlockSpec(memory_space=pltpu.SMEM)


def place():
    sta = lax.axis_index("sta")
    sat = lax.axis_index("sat")
    return sta // NX, sta % NX, sat // 2, sat % 2


def remote(src, dst, send, recv, device):
    return pltpu.make_async_remote_copy(
        src_ref=src,
        dst_ref=dst,
        send_sem=send,
        recv_sem=recv,
        device_id=device,
        device_id_type=MESH,
    )


def greet(peers):
    barrier = pltpu.get_barrier_semaphore()
    for peer in peers:
        pl.semaphore_signal(barrier, inc=1, device_id=peer, device_id_type=MESH)
    pl.semaphore_wait(barrier, len(peers))


def halves(value):
    high = value.astype(BF16)
    low = (value - high.astype(F32)).astype(BF16)
    return high, low


def turned(a, b, precision=None):
    return lax.dot_general(
        a, b, (((1,), (1,)), ((), ())), preferred_element_type=F32, precision=precision
    )


def product(a_high, a_low, b_high, b_low):
    return turned(a_high, b_high) + turned(a_high, b_low) + turned(a_low, b_high)


def ring_start(view, me, buffers, sems, device, slots):
    far, right, left = (me + 2) % 4, (me + 1) % 4, (me + 3) % 4
    b_0, b_1, l_0, l_1, r_0, r_1 = buffers[:6]
    send, recv = sems
    plan = (
        (view(far, 0), b_0, right),
        (view(far, 1), b_1, left),
        (view(right, 1), l_1, right),
        (view(left, 0), r_0, left),
    )
    copies = []
    for slot in slots:
        src, dst, peer = plan[slot]
        copy = remote(src, dst, send.at[slot], recv.at[slot], device(peer))
        copy.start()
        copies.append(copy)
    return copies


def ring_middle(view, me, buffers, sems, device, copies):
    right, left = (me + 1) % 4, (me + 3) % 4
    b_0, b_1, l_0, l_1, r_0, r_1, s_0, s_1 = buffers
    send, recv = sems
    copies[0].wait_recv()
    s_0[...] = view(right, 0)[...] + b_0[...]
    one = remote(s_0, l_0, send.at[4], recv.at[4], device(right))
    one.start()
    copies[1].wait_recv()
    s_1[...] = view(left, 1)[...] + b_1[...]
    two = remote(s_1, r_1, send.at[5], recv.at[5], device(left))
    two.start()
    return copies + [one, two]


def ring_finish(view, me, buffers, copies, out_0, out_1):
    b_0, b_1, l_0, l_1, r_0, r_1 = buffers[:6]
    for index in (2, 3, 4, 5):
        copies[index].wait_recv()
    out_0[...] = view(me, 0)[...] + l_0[...] + r_0[...]
    out_1[...] = view(me, 1)[...] + l_1[...] + r_1[...]


def main_kernel(*refs):
    ids_a, ids_v, orbit = refs[0:3]
    mine = refs[3:8]
    out, out_small = refs[8:10]
    refs = refs[10:]
    other, refs = refs[:5], refs[5:]
    (ids_w, ids_b, full, sv, sd, st, sr, sides, crossed, f_high, f_low, u_high, u_low,
     extra, e_left, normal, own_sum, small), refs = refs[:18], refs[18:]
    bufs, refs = [refs[i * 8 : (i + 1) * 8] for i in range(4)], refs[32:]
    (y_part, x_part, total, arrived, small_y, small_x, small_z, hold_x, hold_z), refs = (
        refs[:9], refs[9:])
    g_send, g_recv, local = refs[:3]
    refs = refs[3:]
    sems = [(refs[2 * i], refs[2 * i + 1]) for i in range(4)]
    z_send, z_recv, s_send, s_recv = refs[8:]
    z, x, y, c = place()

    def at_y(peer):
        return (z * NX + x, peer * 2 + c)

    def at_x(peer):
        return (z * NX + peer, y * 2 + c)

    def at_z(peer):
        return (peer * NX + x, y * 2 + c)

    mate = (z * NX + x, y * 2 + 1 - c)
    far, right, left = (y + 2) % NY, (y + 1) % NY, (y + 3) % NY

    greet(
        [at_y((y + k) % NY) for k in range(1, NY)]
        + [at_x((x + k) % NX) for k in range(1, NX)]
        + [at_z((z + k) % NZ) for k in range(1, NZ)]
        + [mate]
    )

    head, tail = (0, CUT), (CUT, OWN - CUT)

    def base_of(chip, core):
        return (chip * 2 + core) * OWN

    def part(chip, cut):
        return full.at[pl.ds(base_of(chip, c) + cut[0], cut[1])]

    def own(cut):
        return orbit.at[pl.ds(cut[0], cut[1])]

    def go(slot, src, dst, device):
        copy = remote(src, dst, g_send.at[slot], g_recv.at[slot], device)
        copy.start()
        return copy

    right_head = go(0, own(head), part(y, head), at_y(right))
    left_tail = go(1, own(tail), part(y, tail), at_y(left))
    right_tail = go(2, own(tail), part(y, tail), at_y(right))
    left_head = go(3, own(head), part(y, head), at_y(left))
    keep = pltpu.make_async_copy(orbit, full.at[pl.ds(base_of(y, c), OWN)], local.at[0])
    keep.start()
    swaps = [go(6 + i, a, b, mate) for i, (a, b) in enumerate(zip((ids_v,) + mine, (ids_w,) + other))]
    mate_own = go(12, orbit, full.at[pl.ds(base_of(y, c), OWN)], mate)

    extra[...] = jnp.zeros_like(extra)
    sv[:, :, SLOTS:, :] = jnp.zeros((4, 3, 8, EPOCHS), F32)
    sd[:, :, SLOTS:, :] = jnp.zeros((4, 3, 8, EPOCHS), F32)
    crossed[:, SLOTS:] = jnp.zeros((4, 8, PAR, 128), F32)
    lane_rows = lax.broadcasted_iota(jnp.int32, (128, EPOCHS), 0)
    row8 = lax.broadcasted_iota(jnp.int32, (8, EPOCHS), 0)

    def knot_rows(index):
        knots = mine[4] if index < 2 else other[4]
        pick = lane_rows % 32 == knots[index % 2 : index % 2 + 1, :] + KNOTS * index
        return jnp.where(pick & (lane_rows < 96), 1.0, 0.0)

    def prepare(index):
        sight, mapping, residual, counts, _ = mine if index < 2 else other
        s = index % 2
        weight = counts[s].astype(F32)
        path = mapping[s]
        seen = residual[s]
        shared = jnp.maximum(jnp.sum(weight, 0, keepdims=True), 1.0)
        share = 1.0 / shared
        weight_map = weight * path
        sum_map = jnp.sum(weight_map, 0, keepdims=True)
        sum_res = jnp.sum(weight * seen, 0, keepdims=True)
        st[index] = weight * (path - sum_map * share)
        sr[index] = weight * (seen - sum_res * share)
        root = weight * lax.rsqrt(shared)
        other_root = jnp.sqrt(weight)
        for k in range(3):
            sv[index, k, 0:SLOTS] = sight[s, k] * root
            sd[index, k, 0:SLOTS] = sight[s, k] * other_root
        square = jnp.sum(weight_map * path, 0, keepdims=True) - sum_map * sum_map * share
        cross = jnp.sum(weight_map * seen, 0, keepdims=True) - sum_map * sum_res * share
        pair = jnp.where(row8 == 0, square, jnp.where(row8 == 1, cross, 0.0))
        return turned(pair, knot_rows(index), HIGH)

    own_row = lax.broadcasted_iota(jnp.int32, (128, 128), 0) // PAR
    own_lane = lax.broadcasted_iota(jnp.int32, (128, 128), 1) // PAR

    def squeeze(block):
        block = jnp.where(own_row == own_lane, block, 0.0)
        return jnp.sum(block.reshape(16, PAR, 128), 0)

    def build(chip, core, diagonal):
        base = base_of(chip, core)
        top = (chip * 2 + core) * 128

        def one(j, index, table):
            ids = ids_a if index < 2 else ids_b
            slot = ids[index % 2, base + j]
            return (
                table[index, 0, pl.ds(slot, 1), :] * full[base + j, 0]
                + table[index, 1, pl.ds(slot, 1), :] * full[base + j, 1]
                + table[index, 2, pl.ds(slot, 1), :] * full[base + j, 2]
            )

        def fill(k, second):
            row = pl.multiple_of(top + k * 16, 16)
            inner = pl.multiple_of(k * 16, 16)
            for index in range(4):
                lanes = slice(index * EPOCHS, (index + 1) * EPOCHS)
                a = one(2 * k, index, sv)
                b = one(2 * k + 1, index, sv) if second else jnp.zeros_like(a)
                high, low = halves(jnp.concatenate([a, b], axis=0))
                f_high[pl.ds(row, 16), lanes] = high
                f_low[pl.ds(row, 16), lanes] = low
                if diagonal:
                    a = one(2 * k, index, sd)
                    b = one(2 * k + 1, index, sd) if second else jnp.zeros_like(a)
                    high, low = halves(jnp.concatenate([a, b], axis=0))
                    u_high[pl.ds(inner, 16), lanes] = high
                    u_low[pl.ds(inner, 16), lanes] = low

        def step(k, carry):
            fill(k, True)
            return carry

        lax.fori_loop(0, 7, step, 0)
        fill(7, False)
        if diagonal:
            own_sum[chip] = squeeze(product(u_high[...], u_low[...], u_high[...], u_low[...]))

    local_rows = prepare(0) + prepare(1)
    keep.wait()
    for copy in swaps:
        copy.wait_recv()
    hand = pltpu.make_async_copy(ids_w, ids_b, local.at[1])
    hand.start()
    local_rows = local_rows + prepare(2) + prepare(3)
    hand.wait()
    build(y, c, True)
    mates = [mate_own]
    right_head.wait_recv()
    relay_right = go(4, part(left, head), part(left, head), at_y(right))
    mates.append(go(13, part(left, head), part(left, head), mate))
    left_tail.wait_recv()
    relay_left = go(5, part(right, tail), part(right, tail), at_y(left))
    mates.append(go(14, part(right, tail), part(right, tail), mate))
    mate_own.wait_recv()
    build(y, 1 - c, False)
    right_tail.wait_recv()
    mates.append(go(15, part(left, tail), part(left, tail), mate))
    left_head.wait_recv()
    mates.append(go(16, part(right, head), part(right, head), mate))
    build(left, c, True)
    build(right, c, True)
    for copy in mates[1:]:
        copy.wait_recv()
    build(left, 1 - c, False)
    build(right, 1 - c, False)
    relay_right.wait_recv()
    mates.append(go(17, part(far, head), part(far, head), mate))
    relay_left.wait_recv()
    mates.append(go(18, part(far, tail), part(far, tail), mate))
    build(far, c, True)
    for copy in mates[5:]:
        copy.wait_recv()
    build(far, 1 - c, False)

    for index in range(4):
        sight = mine[0] if index < 2 else other[0]
        ids = ids_a if index < 2 else ids_b
        s = index % 2

        def visit(m, carry):
            sat = ids[2 + s, m]
            design = (
                sight[s, 0, pl.ds(m, 1), :] * full[sat, 0]
                + sight[s, 1, pl.ds(m, 1), :] * full[sat, 1]
                + sight[s, 2, pl.ds(m, 1), :] * full[sat, 2]
            )
            sides[m, :, 0:EPOCHS] = design * st[index, pl.ds(m, 1), :]
            sides[m, :, EPOCHS : 2 * EPOCHS] = design * sr[index, pl.ds(m, 1), :]
            return carry

        lax.fori_loop(0, SLOTS, visit, 0, unroll=4)
        high, low = halves(sides[...].reshape(SLOTS * PAR, 2 * EPOCHS))
        last_rows = jnp.where((lane_rows % 32 == 16) & (lane_rows < 96), 1.0, 0.0)
        pickers = jnp.concatenate([knot_rows(index), last_rows], axis=1).astype(BF16)
        crossed[index, 0:SLOTS] = (turned(high, pickers) + turned(low, pickers)).reshape(
            SLOTS, PAR, 128
        )

    def collect(group, carry):
        for j in range(OWN):
            sat = group * OWN + j
            extra[group * 16 + j] = (
                crossed[0, ids_a[0, sat]]
                + crossed[1, ids_a[1, sat]]
                + crossed[2, ids_b[0, sat]]
                + crossed[3, ids_b[1, sat]]
            )
        return carry

    lax.fori_loop(0, NZ, collect, 0)

    lane = lax.broadcasted_iota(jnp.int32, (1, 128), 1)
    scale = jnp.where(lane % 32 < 16, lax.rsqrt(local_rows[0:1] + PRIOR), 0.0)
    special = jnp.where(lane % 32 == 16, -1.0, local_rows[1:2] * scale)
    row = lax.broadcasted_iota(jnp.int32, (8, 128), 0)
    left_scale = jnp.broadcast_to(scale, (1024, 128))
    side = extra[...].reshape(1024, 128) * left_scale
    high, low = halves(side)
    e_left[...] = jnp.where(lane < 64, high.astype(F32), low.astype(F32)).astype(BF16)
    special = jnp.where(row == 0, special, 0.0)
    high, low = halves(special)
    special = jnp.where(lane < 64, high.astype(F32), low.astype(F32))
    e_left[112:128] = jnp.concatenate(
        [e_left[112:128].astype(F32)[0:8], special], axis=0
    ).astype(BF16)
    right_scale = jnp.where(lane % 32 < 16, scale, 1.0)

    def right_side(slab):
        group = slab * 2 + c
        rows = pl.ds(pl.multiple_of(group * 128, 128), 128)
        side = extra[pl.ds(group * 16, 16)].reshape(128, 128) * right_scale
        high, low = halves(side)
        side = jnp.where((lane >= 32) & (lane < 64), low.astype(F32), high.astype(F32))
        return f_high[rows], f_low[rows], side.astype(BF16)

    def multiply(first, count, slabs):
        rows = slice(first * 128, (first + count) * 128)
        sides_of = [right_side(slab) for slab in slabs]
        r_high, r_low, r_side = [
            jnp.concatenate([part[i] for part in sides_of], axis=0) for i in range(3)
        ]
        result = product(f_high[rows], f_low[rows], r_high, r_low) + turned(e_left[rows], r_side)
        for i, slab in enumerate(slabs):
            lanes = slice(i * 128, (i + 1) * 128)
            normal[slab, first : first + count] = -result[:, lanes].reshape(count, 128, 128)

    def rows_of(peer):
        return pl.ds(pl.multiple_of(jnp.minimum(peer * 30 // 8, 10) * 8, 8), COVER)

    a_cut = (pl.ds(0, 3), pl.ds(3, ZA - 3))
    b_cut = (pl.ds(0, 2), pl.ds(2, 1))

    def ay_view(peer, half):
        return normal.at[peer, a_cut[half], pl.ds(0, ROWS)]

    def bx_view(peer, half):
        return normal.at[pl.ds(2 * half, 2), pl.ds(ZA, NZ - ZA), rows_of(peer)]

    def ax_view(peer, half):
        return y_part.at[a_cut[half], rows_of(peer)]

    def by_view(peer, half):
        return x_part.at[peer, b_cut[half]]

    def small_start(base, source, target, me, size, device):
        copies = []
        for k in range(1, size):
            peer = (me + k) % size
            slot = base + k - 1
            copy = remote(
                source(peer), target.at[me], s_send.at[slot], s_recv.at[slot], device(peer)
            )
            copy.start()
            copies.append(copy)
        return copies

    def small_sum(copies, target, me, own, size):
        target[me] = own
        for copy in copies:
            copy.wait_recv()
        result = target[0]
        for k in range(1, size):
            result = result + target[k]
        return result

    multiply(0, 3, (far, right))
    ay = ring_start(ay_view, y, bufs[0], sems[0], at_y, (0,))
    multiply(3, ZA - 3, (far, right))
    ay += ring_start(ay_view, y, bufs[0], sems[0], at_y, (1, 2))
    multiply(ZA, NZ - ZA, (far, right))
    multiply(ZA, NZ - ZA, (left, y))
    bx = ring_start(bx_view, x, bufs[1], sems[1], at_x, (0, 1, 2, 3))
    multiply(0, 3, (left, y))
    ay += ring_start(ay_view, y, bufs[0], sems[0], at_y, (3,))
    multiply(3, ZA - 3, (left, y))

    for slab in range(NY):
        small[slab, 0:8] = own_sum[slab] + squeeze(normal[slab, slab * 2 + c])
        small[slab, 8:16] = normal[slab, 0, ROWS : ROWS + 8, :]
    sy = small_start(0, lambda peer: small.at[peer], small_y, y, NY, at_y)

    ay = ring_middle(ay_view, y, bufs[0], sems[0], at_y, ay)
    bx = ring_middle(bx_view, x, bufs[1], sems[1], at_x, bx)

    hold_x[...] = small_sum(sy, small_y, y, small[y], NY)
    sx = small_start(3, lambda peer: hold_x, small_x, x, NX, at_x)

    ring_finish(ay_view, y, bufs[0], ay, y_part.at[a_cut[0]], y_part.at[a_cut[1]])
    ax = ring_start(ax_view, x, bufs[2], sems[2], at_x, (0, 1, 2, 3))
    ring_finish(
        bx_view, x, bufs[1], bx, x_part.at[pl.ds(0, 2)], x_part.at[pl.ds(2, 2)]
    )
    by = ring_start(by_view, y, bufs[3], sems[3], at_y, (0, 1, 2, 3))

    hold_z[...] = small_sum(sx, small_x, x, hold_x[...], NX)
    sz = small_start(6, lambda peer: hold_z, small_z, z, NZ, at_z)

    ax = ring_middle(ax_view, x, bufs[2], sems[2], at_x, ax)
    by = ring_middle(by_view, y, bufs[3], sems[3], at_y, by)
    ring_finish(ax_view, x, bufs[2], ax, total.at[pl.ds(0, 3)], total.at[pl.ds(3, ZA - 3)])
    ring_finish(by_view, y, bufs[3], by, total.at[pl.ds(ZA, 2)], total.at[pl.ds(ZA + 2, 1)])

    final = []
    for k in (4, 3, 5, 2, 6, 1, 7):
        peer = (z + k) % NZ
        copy = remote(
            total.at[peer], arrived.at[k - 1], z_send.at[k - 1], z_recv.at[k - 1], at_z(peer)
        )
        copy.start()
        final.append((k, copy))
    out_small[...] = small_sum(sz, small_z, z, hold_z[...], NZ)
    value = total[z]
    for k, copy in reversed(final):
        copy.wait_recv()
        value = value + arrived[k - 1]
    out[...] = value
    sent = [right_head, left_tail, right_tail, left_head, relay_right, relay_left]
    for copies in (sent, swaps, mates, sy, sx, sz, ay, bx, ax, by):
        for copy in copies:
            copy.wait_send()
    for k, copy in final:
        copy.wait_send()


def finish_kernel(block, sums, owned, right, blocks):
    z, x, y, c = place()
    skip = x * 30 - jnp.minimum(x * 30 // 8, 10) * 8
    cross_factor = SATS / math.sqrt(512 * EPOCHS)
    factor = SATS / (512 * SLOTS * EPOCHS)
    value = pltpu.roll(block[...], COVER - skip, 0)[0:30, 0:ROWS]
    row = (z * NX + x) * 30 + lax.broadcasted_iota(jnp.int32, (30, ROWS), 0)
    column = (y * 2 + c) * ROWS + lax.broadcasted_iota(jnp.int32, (30, ROWS), 1)
    owned[...] = jnp.where(row // PAR == column // PAR, 0.0, value) * cross_factor
    right[...] = sums[8:9, 0:ROWS] * factor
    scaled = sums[0:8] * factor
    for j in range(OWN):
        blocks[j] = scaled[:, j * PAR : (j + 1) * PAR]


def ring_buffers(half_0, half_1):
    shapes = [half_0, half_1, half_0, half_1, half_0, half_1, half_0, half_1]
    return [pltpu.VMEM(shape, F32) for shape in shapes]


def shards(sight, mapping, residual, counts, track, knots, orbit):
    shape = jax.ShapeDtypeStruct
    stations = (sight, mapping, residual, counts, knots)
    hit = track[:, :, None] == jnp.arange(128, dtype=jnp.int32)[None, None, :]
    offset = jnp.arange(SLOTS, dtype=jnp.int32)[None, :, None] - SLOTS
    slots = SLOTS + jnp.sum(jnp.where(hit, offset, 0), axis=1)
    ids = jnp.concatenate([slots, jnp.pad(track, ((0, 0), (0, 128 - SLOTS)))], axis=0)

    nb = NZ - ZA
    scratch = (
        [pltpu.VMEM(a.shape, a.dtype) for a in stations]
        + [
            pltpu.VMEM((4, 128), jnp.int32),
            pltpu.SMEM((4, 128), jnp.int32),
            pltpu.VMEM((SATS, 3, PAR, EPOCHS), F32),
            pltpu.VMEM((4, 3, SLOTS + 8, EPOCHS), F32),
            pltpu.VMEM((4, 3, SLOTS + 8, EPOCHS), F32),
            pltpu.VMEM((4, SLOTS, EPOCHS), F32),
            pltpu.VMEM((4, SLOTS, EPOCHS), F32),
            pltpu.VMEM((SLOTS, PAR, 2 * EPOCHS), F32),
            pltpu.VMEM((4, SLOTS + 8, PAR, 128), F32),
            pltpu.VMEM((1024, 4 * EPOCHS), BF16),
            pltpu.VMEM((1024, 4 * EPOCHS), BF16),
            pltpu.VMEM((128, 4 * EPOCHS), BF16),
            pltpu.VMEM((128, 4 * EPOCHS), BF16),
            pltpu.VMEM((128, PAR, 128), F32),
            pltpu.VMEM((1024, 128), BF16),
            pltpu.VMEM((NY, NZ, 128, 128), F32),
            pltpu.VMEM((NY, PAR, 128), F32),
            pltpu.VMEM((NY, 16, 128), F32),
        ]
        + ring_buffers((3, ROWS, 128), (ZA - 3, ROWS, 128))
        + ring_buffers((2, nb, COVER, 128), (2, nb, COVER, 128))
        + ring_buffers((3, COVER, 128), (ZA - 3, COVER, 128))
        + ring_buffers((2, COVER, 128), (1, COVER, 128))
        + [
            pltpu.VMEM((ZA, ROWS, 128), F32),
            pltpu.VMEM((NY, nb, COVER, 128), F32),
            pltpu.VMEM((NZ, COVER, 128), F32),
            pltpu.VMEM((NZ - 1, COVER, 128), F32),
            pltpu.VMEM((NY, 16, 128), F32),
            pltpu.VMEM((NX, 16, 128), F32),
            pltpu.VMEM((NZ, 16, 128), F32),
            pltpu.VMEM((16, 128), F32),
            pltpu.VMEM((16, 128), F32),
            pltpu.SemaphoreType.DMA((19,)),
            pltpu.SemaphoreType.DMA((19,)),
            pltpu.SemaphoreType.DMA((2,)),
        ]
        + [pltpu.SemaphoreType.DMA((6,))] * 8
        + [
            pltpu.SemaphoreType.DMA((7,)),
            pltpu.SemaphoreType.DMA((7,)),
            pltpu.SemaphoreType.DMA((13,)),
            pltpu.SemaphoreType.DMA((13,)),
        ]
    )
    block, sums = pl.pallas_call(
        main_kernel,
        name="network",
        out_shape=[shape((COVER, 128), F32), shape((16, 128), F32)],
        in_specs=[SMEM] + [VMEM] * 7,
        out_specs=[VMEM, VMEM],
        scratch_shapes=scratch,
        compiler_params=pltpu.CompilerParams(
            collective_id=0, has_side_effects=True, vmem_limit_bytes=60 * 1024 * 1024
        ),
    )(ids, ids, orbit, *stations)

    owned, right, blocks = pl.pallas_call(
        finish_kernel,
        name="finish",
        out_shape=[
            shape((30, ROWS), F32),
            shape((1, ROWS), F32),
            shape((OWN, PAR, PAR), F32),
        ],
        in_specs=[VMEM, VMEM],
        out_specs=[VMEM] * 3,
    )(block, sums)
    return owned.T, right.reshape(ROWS), blocks


def solution(mesh):
    placed = (
        P(("sta", "sat"), None, None, None),
        P(("sta", "sat"), None, None),
        P(("sta", "sat"), None, None),
        P(("sta", "sat"), None, None),
        P(("sta", "sat"), None),
        P(("sta", "sat"), None),
        P("sat", None, None, None),
    )
    return jax.shard_map(
        shards,
        mesh=mesh,
        in_specs=placed,
        out_specs=(P("sat", "sta"), P("sat"), P("sat", None, None)),
        check_vma=False,
    )
```

time: 80.5 us -> 64 us (0.80); the launches traced: 80.2 us -> 62.8 us
  Pallas kernels: 75.3 us -> 59.2 us
  other arithmetic: 3.31 us -> 0.69 us
  local copies, waits for them, and re-layouts: 0.82 us -> 2.22 us
    pallas_call x3 -> x2, Pallas kernels: 75.3 us -> 59.2 us  [the longest x1 57.8 us: shards(): pl.pallas_call(main_kernel, name='network', out_shape=[shape((COVER, 128)...]
    mul x3 -> x0, other arithmetic: 3.29 us -> none  [the longest x1 1.41 us: shards(): cross_part = jnp.where(row == column, 0.0, owned) * cross_factor]
    unnamed x1 -> x3, local copies, waits for them, and re-layouts: 0.73 us -> 2.22 us
where the time goes in v2:
time: 64 us; the launch traced here: 62.8 us
  Pallas kernels  59.2 us (92%)
  local copies, waits for them, and re-layouts  2.22 us (3%)
  other arithmetic  0.69 us (1%)
  between operations  0.66 us (1%)
    pallas_call x1, Pallas kernels, shards(): pl.pallas_call(main_kernel, name='network', out_shape=[shape((COVER, 128)...  57.8 us
    unnamed x3, local copies, waits for them, and re-layouts  2.22 us
    pallas_call x1, Pallas kernels, shards(): pl.pallas_call(finish_kernel, name='finish', out_shape=[shape((30, ROWS),...  1.43 us

profile of v2, /device:TPU:2, one launch (start us, length us, event | category | flops | bytes accessed | tf_op | source)
XLA Modules:
  0.0 62.8 jit_solution(2983233948248365812)
XLA Ops:
  0.6 0.0 copy-start
  0.7 0.7 %copy-done = s32[2,32]{1,0:T(2,128)S(1)} copy-done((s32[2,32]{1,0:T(2,128)S(1)}, s32[2,32]{1,0:T(2,128)}, u32[]{:S(2)}) %copy-start) | copy-done | bytes 280
  1.3 0.1 select_reduce_fusion
  1.4 0.6 pad_add_fusion.refs_0_.refs_1_
  2.0 57.8 %network.1 = (f32[40,128]{1,0:T(8,128)}, f32[16,128]{1,0:T(8,128)}) custom-call(s32[4,128]{1,0:T(4,128)} %pad_add_fusion.refs_0_.refs_1_, s32[4,128]{1,0:T(4,128)} %pad_add_fusion.refs_0_.refs_1_, f32[15,3,8,256]{3,2,1,0:T(8,128)} %refs_2_.1, f32[2,3,32,256]{3,2,1,0:T(8,128)} %refs_3_.1, f32[2,32,256]{2,1,0:T(8,128)} %refs_4_.1, f32[2,32,256]{2,1,0:T(8,128)} %refs_5_.1, ...), custom_call_target="tpu_custom_call" | custom-call | tf_op jit(solution)/shard_map/network/pallas_call | solution.py:543
  59.8 1.4 %finish.1 = (f32[30,120]{1,0:T(8,128)}, f32[1,120]{1,0:T(1,128)}, f32[15,8,8]{2,1,0:T(8,128)}) custom-call(f32[40,128]{1,0:T(8,128)} %get-tuple-element.8.block, f32[16,128]{1,0:T(8,128)} %get-tuple-element.9.sums), custom_call_target="tpu_custom_call" | custom-call | tf_op jit(solution)/shard_map/finish/pallas_call | solution.py:555
  61.3 1.6 %copy.11 = f32[15,8,8]{0,2,1:T(8,128)} copy(f32[15,8,8]{2,1,0:T(8,128)} %get-tuple-element.18) | data formatting | bytes 7680
  (2 shorter events, 0.0 us)
Async XLA Ops:
  0.6 0.7 %copy-start = (s32[2,32]{1,0:T(2,128)S(1)}, s32[2,32]{1,0:T(2,128)}, u32[]{:S(2)}) copy-start(s32[2,32]{1,0:T(2,128)} %param.11) | copy-start | bytes 772

commit v3 on v2

v3 whole, which is shorter than its diff:
```python
import functools
import math

import jax
import jax.numpy as jnp
from jax import lax
from jax.experimental import pallas as pl
from jax.experimental.pallas import tpu as pltpu
from jax.sharding import PartitionSpec as P

F32 = jnp.float32
BF16 = jnp.bfloat16
MESH = pl.DeviceIdType.MESH
HIGH = lax.Precision.HIGHEST

SATS = 120
OWN = 15
PAR = 8
SLOTS = 32
EPOCHS = 256
KNOTS = 4
PRIOR = 1.0
NY = 4
NX = 4
NZ = 8
ROWS = 120
COVER = 40
CUT = 8
ZA = 5
ANY = pl.BlockSpec(memory_space=pl.ANY)
VMEM = pl.BlockSpec(memory_space=pltpu.VMEM)
SMEM = pl.BlockSpec(memory_space=pltpu.SMEM)


def place():
    sta = lax.axis_index("sta")
    sat = lax.axis_index("sat")
    return sta // NX, sta % NX, sat // 2, sat % 2


def remote(src, dst, send, recv, device):
    return pltpu.make_async_remote_copy(
        src_ref=src,
        dst_ref=dst,
        send_sem=send,
        recv_sem=recv,
        device_id=device,
        device_id_type=MESH,
    )


def greet(peers):
    barrier = pltpu.get_barrier_semaphore()
    for peer in peers:
        pl.semaphore_signal(barrier, inc=1, device_id=peer, device_id_type=MESH)
    pl.semaphore_wait(barrier, len(peers))


def halves(value):
    high = value.astype(BF16)
    low = (value - high.astype(F32)).astype(BF16)
    return high, low


def turned(a, b, precision=None):
    return lax.dot_general(
        a, b, (((1,), (1,)), ((), ())), preferred_element_type=F32, precision=precision
    )


def product(a_high, a_low, b_high, b_low):
    return turned(a_high, b_high) + turned(a_high, b_low) + turned(a_low, b_high)


def ring_start(view, me, buffers, sems, device, slots):
    far, right, left = (me + 2) % 4, (me + 1) % 4, (me + 3) % 4
    b_0, b_1, l_0, l_1, r_0, r_1 = buffers[:6]
    send, recv = sems
    plan = (
        (view(far, 0), b_0, right),
        (view(far, 1), b_1, left),
        (view(right, 1), l_1, right),
        (view(left, 0), r_0, left),
    )
    copies = []
    for slot in slots:
        src, dst, peer = plan[slot]
        copy = remote(src, dst, send.at[slot], recv.at[slot], device(peer))
        copy.start()
        copies.append(copy)
    return copies


def ring_middle(view, me, buffers, sems, device, copies):
    right, left = (me + 1) % 4, (me + 3) % 4
    b_0, b_1, l_0, l_1, r_0, r_1, s_0, s_1 = buffers
    send, recv = sems
    copies[0].wait_recv()
    s_0[...] = view(right, 0)[...] + b_0[...]
    one = remote(s_0, l_0, send.at[4], recv.at[4], device(right))
    one.start()
    copies[1].wait_recv()
    s_1[...] = view(left, 1)[...] + b_1[...]
    two = remote(s_1, r_1, send.at[5], recv.at[5], device(left))
    two.start()
    return copies + [one, two]


def ring_finish(view, me, buffers, copies, out_0, out_1):
    b_0, b_1, l_0, l_1, r_0, r_1 = buffers[:6]
    for index in (2, 3, 4, 5):
        copies[index].wait_recv()
    out_0[...] = view(me, 0)[...] + l_0[...] + r_0[...]
    out_1[...] = view(me, 1)[...] + l_1[...] + r_1[...]


def main_kernel(*refs):
    track, orbit = refs[0:2]
    given = refs[2:7]
    out, out_small = refs[7:9]
    refs = refs[9:]
    mine, other, refs = refs[:5], refs[5:10], refs[10:]
    (track_s, ids_v, ids_w, ids_a, ids_b, full, sv, factors, f_high, f_low, u_high, u_low,
     t_high, t_low, pick, e_left, e_right, normal, own_sum, small), refs = refs[:20], refs[20:]
    bufs, refs = [refs[i * 8 : (i + 1) * 8] for i in range(6)], refs[48:]
    (y_part, x_part, total, arrived, small_y, small_x, small_z, hold_x, hold_z), refs = (
        refs[:9], refs[9:])
    g_send, g_recv, local = refs[:3]
    refs = refs[3:]
    sems = [(refs[2 * i], refs[2 * i + 1]) for i in range(6)]
    z_send, z_recv, s_send, s_recv = refs[12:]
    z, x, y, c = place()

    def at_y(peer):
        return (z * NX + x, peer * 2 + c)

    def at_x(peer):
        return (z * NX + peer, y * 2 + c)

    def at_z(peer):
        return (peer * NX + x, y * 2 + c)

    mate = (z * NX + x, y * 2 + 1 - c)
    far, right, left = (y + 2) % NY, (y + 1) % NY, (y + 3) % NY
    head, tail = (0, CUT), (CUT, OWN - CUT)

    def base_of(chip, core):
        return (chip * 2 + core) * OWN

    def part(chip, cut):
        return full.at[pl.ds(base_of(chip, c) + cut[0], cut[1])]

    def own(cut):
        return orbit.at[pl.ds(cut[0], cut[1])]

    keeps = [
        pltpu.make_async_copy(a, b, local.at[i])
        for i, (a, b) in enumerate(
            zip(
                (track,) + given + (orbit,),
                (track_s,) + mine + (full.at[pl.ds(base_of(y, c), OWN)],),
            )
        )
    ]
    for copy in keeps:
        copy.start()

    greet(
        [at_y((y + k) % NY) for k in range(1, NY)]
        + [at_x((x + k) % NX) for k in range(1, NX)]
        + [at_z((z + k) % NZ) for k in range(1, NZ)]
        + [mate]
    )

    def go(slot, src, dst, device):
        copy = remote(src, dst, g_send.at[slot], g_recv.at[slot], device)
        copy.start()
        return copy

    right_head = go(0, own(head), part(y, head), at_y(right))
    left_tail = go(1, own(tail), part(y, tail), at_y(left))
    right_tail = go(2, own(tail), part(y, tail), at_y(right))
    left_head = go(3, own(head), part(y, head), at_y(left))
    swaps = [go(7 + i, a, b, mate) for i, (a, b) in enumerate(zip(given, other))]
    mate_own = go(12, orbit, full.at[pl.ds(base_of(y, c), OWN)], mate)

    keeps[0].wait()
    place_lane = lax.broadcasted_iota(jnp.int32, (1, 128), 1)
    for s in range(2):
        slots = jnp.full((1, 128), SLOTS, jnp.int32)
        for m in range(SLOTS):
            slots = jnp.where(place_lane == track_s[s, m], m, slots)
        ids_v[s : s + 1, :] = slots
    hand_a = pltpu.make_async_copy(ids_v, ids_a, local.at[7])
    hand_a.start()
    swaps.append(go(6, ids_v, ids_w, mate))

    blank = jnp.zeros((4, 3, 8, EPOCHS), F32)
    sv[:, :, SLOTS:, :] = blank
    factors[:, :, SLOTS:, :] = blank
    lane_rows = lax.broadcasted_iota(jnp.int32, (128, EPOCHS), 0)
    row8 = lax.broadcasted_iota(jnp.int32, (8, EPOCHS), 0)
    pick_last = jnp.where((lane_rows % 32 == 16) & (lane_rows < 96), 1.0, 0.0).astype(BF16)

    def prepare(index):
        sight, mapping, residual, counts, knots = mine if index < 2 else other
        s = index % 2
        chosen = lane_rows % 32 == knots[s : s + 1, :] + KNOTS * index
        chosen = jnp.where(chosen & (lane_rows < 96), 1.0, 0.0)
        wide = 2 * EPOCHS * index
        pick[:, wide : wide + EPOCHS] = chosen.astype(BF16)
        pick[:, wide + EPOCHS : wide + 2 * EPOCHS] = pick_last
        weight = counts[s].astype(F32)
        path = mapping[s]
        seen = residual[s]
        shared = jnp.maximum(jnp.sum(weight, 0, keepdims=True), 1.0)
        share = 1.0 / shared
        root = lax.rsqrt(shared)
        grow = shared * root
        weight_map = weight * path
        sum_map = jnp.sum(weight_map, 0, keepdims=True)
        sum_res = jnp.sum(weight * seen, 0, keepdims=True)
        scaled = weight * root
        for k in range(3):
            sv[index, k, 0:SLOTS] = sight[s, k] * scaled
        factors[index, 0, 0:SLOTS] = jnp.where(
            weight > 0.0, lax.rsqrt(jnp.maximum(weight, 1.0)) * grow, 0.0
        )
        factors[index, 1, 0:SLOTS] = (path - sum_map * share) * grow
        factors[index, 2, 0:SLOTS] = (seen - sum_res * share) * grow
        square = jnp.sum(weight_map * path, 0, keepdims=True) - sum_map * sum_map * share
        cross = jnp.sum(weight_map * seen, 0, keepdims=True) - sum_map * sum_res * share
        pair = jnp.where(row8 == 0, square, jnp.where(row8 == 1, cross, 0.0))
        return turned(pair, chosen, HIGH)

    own_row = lax.broadcasted_iota(jnp.int32, (128, 128), 0) // PAR
    own_lane = lax.broadcasted_iota(jnp.int32, (128, 128), 1) // PAR
    lane = lax.broadcasted_iota(jnp.int32, (1, 128), 1)

    def squeeze(block):
        block = jnp.where(own_row == own_lane, block, 0.0)
        return jnp.sum(block.reshape(16, PAR, 128), 0)

    def build(chip, core, sides, diagonal):
        base = base_of(chip, core)
        group = chip * 2 + core
        top = group * 128

        def one(j, index):
            ids = ids_a if index < 2 else ids_b
            slot = ids[index % 2, base + j]
            value = (
                sv[index, 0, pl.ds(slot, 1), :] * full[base + j, 0]
                + sv[index, 1, pl.ds(slot, 1), :] * full[base + j, 1]
                + sv[index, 2, pl.ds(slot, 1), :] * full[base + j, 2]
            )
            times = [
                value * factors[index, k, pl.ds(slot, 1), :]
                for k in range(3)
                if (diagonal if k == 0 else sides)
            ]
            return [value] + times

        def fill(k, second):
            row = pl.multiple_of(top + k * 16, 16)
            inner = pl.multiple_of(k * 16, 16)
            for index in range(4):
                lanes = slice(index * EPOCHS, (index + 1) * EPOCHS)
                a = one(2 * k, index)
                b = one(2 * k + 1, index) if second else [jnp.zeros_like(i) for i in a]
                pieces = [halves(jnp.concatenate([i, j], axis=0)) for i, j in zip(a, b)]
                if sides:
                    f_high[pl.ds(row, 16), lanes], f_low[pl.ds(row, 16), lanes] = pieces[0]
                if diagonal:
                    u_high[pl.ds(inner, 16), lanes], u_low[pl.ds(inner, 16), lanes] = pieces[1]
                if sides:
                    wide = 2 * EPOCHS * index
                    for i in range(2):
                        lanes = slice(wide + i * EPOCHS, wide + (i + 1) * EPOCHS)
                        high, low = pieces[i - 2]
                        t_high[pl.ds(inner, 16), lanes] = high
                        t_low[pl.ds(inner, 16), lanes] = low

        def step(k, carry):
            fill(k, True)
            return carry

        lax.fori_loop(0, 7, step, 0)
        fill(7, False)
        if sides:
            side = turned(t_high[...], pick[...]) + turned(t_low[...], pick[...])
            rows = pl.ds(pl.multiple_of(top, 128), 128)
            high, low = halves(side * scale)
            high, low = high.astype(F32), low.astype(F32)
            e_left[rows] = jnp.where(lane < 64, high, low).astype(BF16)
            high, low = halves(side * right_scale)
            high, low = high.astype(F32), low.astype(F32)
            e_right[rows] = jnp.where((lane >= 32) & (lane < 64), low, high).astype(BF16)
        if diagonal:
            own_sum[chip] = squeeze(product(u_high[...], u_low[...], u_high[...], u_low[...]))

    for copy in keeps[1:]:
        copy.wait()
    hand_a.wait()
    local_rows = prepare(0) + prepare(1)
    for copy in swaps:
        copy.wait_recv()
    hand_b = pltpu.make_async_copy(ids_w, ids_b, local.at[8])
    hand_b.start()
    local_rows = local_rows + prepare(2) + prepare(3)
    scale = jnp.where(lane % 32 < 16, lax.rsqrt(local_rows[0:1] + PRIOR), 0.0)
    right_scale = jnp.where(lane % 32 < 16, scale, 1.0)
    special = jnp.where(lane % 32 == 16, -1.0, local_rows[1:2] * scale)
    hand_b.wait()
    build(y, c, True, True)
    mates = [mate_own]
    right_head.wait_recv()
    relay_right = go(4, part(left, head), part(left, head), at_y(right))
    mates.append(go(13, part(left, head), part(left, head), mate))
    left_tail.wait_recv()
    relay_left = go(5, part(right, tail), part(right, tail), at_y(left))
    mates.append(go(14, part(right, tail), part(right, tail), mate))
    mate_own.wait_recv()
    build(y, 1 - c, True, False)
    right_tail.wait_recv()
    mates.append(go(15, part(left, tail), part(left, tail), mate))
    left_head.wait_recv()
    mates.append(go(16, part(right, head), part(right, head), mate))
    build(left, c, True, True)
    build(right, c, True, True)
    for copy in mates[1:]:
        copy.wait_recv()
    build(left, 1 - c, True, False)
    build(right, 1 - c, True, False)
    relay_right.wait_recv()
    mates.append(go(17, part(far, head), part(far, head), mate))
    relay_left.wait_recv()
    mates.append(go(18, part(far, tail), part(far, tail), mate))
    build(far, c, True, False)
    for copy in mates[5:]:
        copy.wait_recv()
    build(far, 1 - c, True, False)

    row = lax.broadcasted_iota(jnp.int32, (8, 128), 0)
    high, low = halves(jnp.where(row == 0, special, 0.0))
    special = jnp.where(lane < 64, high.astype(F32), low.astype(F32))
    e_left[112:128] = jnp.concatenate(
        [e_left[112:128].astype(F32)[0:8], special], axis=0
    ).astype(BF16)

    def multiply(first, count, slabs):
        rows = slice(first * 128, (first + count) * 128)
        own_rows = [pl.ds(pl.multiple_of((slab * 2 + c) * 128, 128), 128) for slab in slabs]
        r_high, r_low, r_side = [
            jnp.concatenate([ref[i] for i in own_rows], axis=0)
            for ref in (f_high, f_low, e_right)
        ]
        result = product(f_high[rows], f_low[rows], r_high, r_low) + turned(e_left[rows], r_side)
        for i, slab in enumerate(slabs):
            lanes = slice(i * 128, (i + 1) * 128)
            normal[slab, first : first + count] = -result[:, lanes].reshape(count, 128, 128)

    def rows_of(peer):
        return pl.ds(pl.multiple_of(jnp.minimum(peer * 30 // 8, 10) * 8, 8), COVER)

    row_cut = (pl.ds(0, 64), pl.ds(64, ROWS - 64))
    cuts = ((pl.ds(0, 2), pl.ds(2, 1)), (pl.ds(3, 1), pl.ds(4, 1)))
    b_cut = (pl.ds(0, 2), pl.ds(2, 1))

    def first_view(which):
        zs = (pl.ds(0, 3), pl.ds(3, 2))[which]
        return lambda peer, half: normal.at[peer, zs, row_cut[half]]

    def second_view(which):
        return lambda peer, half: y_part.at[cuts[which][half], rows_of(peer)]

    def bx_view(peer, half):
        return normal.at[pl.ds(2 * half, 2), pl.ds(ZA, NZ - ZA), rows_of(peer)]

    def by_view(peer, half):
        return x_part.at[peer, b_cut[half]]

    def small_start(base, source, target, me, size, device):
        copies = []
        for k in range(1, size):
            peer = (me + k) % size
            slot = base + k - 1
            copy = remote(
                source(peer), target.at[me], s_send.at[slot], s_recv.at[slot], device(peer)
            )
            copy.start()
            copies.append(copy)
        return copies

    def small_sum(copies, target, me, own, size):
        target[me] = own
        for copy in copies:
            copy.wait_recv()
        result = target[0]
        for k in range(1, size):
            result = result + target[k]
        return result

    def last_copy(peer, slot):
        return remote(
            total.at[peer], arrived.at[slot], z_send.at[peer], z_recv.at[slot], at_z(peer)
        )

    def send_last(peers):
        for peer in peers:
            @pl.when(z != peer)
            def _():
                last_copy(peer, z).start()

    a_1, a_2 = first_view(0), first_view(1)
    multiply(0, 3, (far, right))
    ay_1 = ring_start(a_1, y, bufs[0], sems[0], at_y, (0, 1, 2))
    multiply(3, 2, (far, right))
    ay_2 = ring_start(a_2, y, bufs[1], sems[1], at_y, (0, 1, 2))
    multiply(ZA, NZ - ZA, (far, right))
    multiply(ZA, NZ - ZA, (left, y))
    bx = ring_start(bx_view, x, bufs[2], sems[2], at_x, (0, 1, 2, 3))
    multiply(0, 3, (left, y))
    ay_1 += ring_start(a_1, y, bufs[0], sems[0], at_y, (3,))
    multiply(3, 2, (left, y))
    ay_2 += ring_start(a_2, y, bufs[1], sems[1], at_y, (3,))
    ay_1 = ring_middle(a_1, y, bufs[0], sems[0], at_y, ay_1)

    build(far, c, False, True)
    for slab in range(NY):
        small[slab, 0:8] = own_sum[slab] + squeeze(normal[slab, slab * 2 + c])
        small[slab, 8:16] = normal[slab, 0, ROWS : ROWS + 8, :]
    sy = small_start(0, lambda peer: small.at[peer], small_y, y, NY, at_y)

    ay_2 = ring_middle(a_2, y, bufs[1], sems[1], at_y, ay_2)
    bx = ring_middle(bx_view, x, bufs[2], sems[2], at_x, bx)

    c_1, c_2 = second_view(0), second_view(1)
    ring_finish(
        a_1, y, bufs[0], ay_1, y_part.at[pl.ds(0, 3), row_cut[0]], y_part.at[pl.ds(0, 3), row_cut[1]]
    )
    ax_1 = ring_start(c_1, x, bufs[3], sems[3], at_x, (0, 1, 2, 3))

    hold_x[...] = small_sum(sy, small_y, y, small[y], NY)
    sx = small_start(3, lambda peer: hold_x, small_x, x, NX, at_x)

    ring_finish(bx_view, x, bufs[2], bx, x_part.at[pl.ds(0, 2)], x_part.at[pl.ds(2, 2)])
    by = ring_start(by_view, y, bufs[4], sems[4], at_y, (0, 1, 2, 3))
    ax_1 = ring_middle(c_1, x, bufs[3], sems[3], at_x, ax_1)
    ring_finish(
        a_2, y, bufs[1], ay_2, y_part.at[pl.ds(3, 2), row_cut[0]], y_part.at[pl.ds(3, 2), row_cut[1]]
    )
    ax_2 = ring_start(c_2, x, bufs[5], sems[5], at_x, (0, 1, 2, 3))

    hold_z[...] = small_sum(sx, small_x, x, hold_x[...], NX)
    sz = small_start(6, lambda peer: hold_z, small_z, z, NZ, at_z)

    by = ring_middle(by_view, y, bufs[4], sems[4], at_y, by)
    ax_2 = ring_middle(c_2, x, bufs[5], sems[5], at_x, ax_2)
    ring_finish(c_1, x, bufs[3], ax_1, total.at[pl.ds(0, 2)], total.at[pl.ds(2, 1)])
    send_last((0, 1, 2))
    ring_finish(by_view, y, bufs[4], by, total.at[pl.ds(ZA, 2)], total.at[pl.ds(ZA + 2, 1)])
    send_last((5, 6, 7))
    ring_finish(c_2, x, bufs[5], ax_2, total.at[pl.ds(3, 1)], total.at[pl.ds(4, 1)])
    send_last((3, 4))

    out_small[...] = small_sum(sz, small_z, z, hold_z[...], NZ)
    value = total[z]
    for k in (1, 7, 2, 6, 3, 5, 4):
        peer = (z + k) % NZ
        last_copy(peer, peer).wait_recv()
        value = value + arrived[peer]
    out[...] = value
    sent = [right_head, left_tail, right_tail, left_head, relay_right, relay_left]
    for copies in (sent, swaps, mates, sy, sx, sz, ay_1, ay_2, bx, ax_1, by, ax_2):
        for copy in copies:
            copy.wait_send()
    for k in range(1, NZ):
        last_copy((z + k) % NZ, z).wait_send()


def finish_kernel(block, sums, owned, right, blocks):
    z, x, y, c = place()
    skip = x * 30 - jnp.minimum(x * 30 // 8, 10) * 8
    cross_factor = SATS / math.sqrt(512 * EPOCHS)
    factor = SATS / (512 * SLOTS * EPOCHS)
    value = pltpu.roll(block[...], COVER - skip, 0)[0:30, 0:ROWS]
    row = (z * NX + x) * 30 + lax.broadcasted_iota(jnp.int32, (30, ROWS), 0)
    column = (y * 2 + c) * ROWS + lax.broadcasted_iota(jnp.int32, (30, ROWS), 1)
    owned[...] = jnp.where(row // PAR == column // PAR, 0.0, value) * cross_factor
    right[...] = sums[8:9, 0:ROWS] * factor
    scaled = jnp.broadcast_to((sums[0:8] * factor)[:, None, :], (PAR, PAR, 128))
    place_of = lax.broadcasted_iota(jnp.int32, (PAR, PAR, 128), 2) % PAR
    inner = lax.broadcasted_iota(jnp.int32, (PAR, PAR, 128), 1)
    rows = jnp.where(place_of == inner, scaled, 0.0).reshape(PAR * PAR, 128)
    to = lax.broadcasted_iota(jnp.int32, (128, 128), 0)
    lane = lax.broadcasted_iota(jnp.int32, (128, 128), 1)
    moved = turned(rows, jnp.where(to == lane // PAR, 1.0, 0.0), HIGH)
    blocks[...] = moved.reshape(PAR, PAR, 128)[:, :, 0:OWN]


def ring_buffers(half_0, half_1):
    shapes = [half_0, half_1, half_0, half_1, half_0, half_1, half_0, half_1]
    return [pltpu.VMEM(shape, F32) for shape in shapes]


def shards(sight, mapping, residual, counts, track, knots, orbit):
    shape = jax.ShapeDtypeStruct
    stations = (sight, mapping, residual, counts, knots)
    nb = NZ - ZA
    big = 4 * EPOCHS
    scratch = (
        [pltpu.VMEM(a.shape, a.dtype) for a in stations] * 2
        + [
            pltpu.SMEM((2, SLOTS), jnp.int32),
            pltpu.VMEM((2, 128), jnp.int32),
            pltpu.VMEM((2, 128), jnp.int32),
            pltpu.SMEM((2, 128), jnp.int32),
            pltpu.SMEM((2, 128), jnp.int32),
            pltpu.VMEM((SATS, 3, PAR, EPOCHS), F32),
            pltpu.VMEM((4, 3, SLOTS + 8, EPOCHS), F32),
            pltpu.VMEM((4, 3, SLOTS + 8, EPOCHS), F32),
            pltpu.VMEM((1024, big), BF16),
            pltpu.VMEM((1024, big), BF16),
            pltpu.VMEM((128, big), BF16),
            pltpu.VMEM((128, big), BF16),
            pltpu.VMEM((128, 2 * big), BF16),
            pltpu.VMEM((128, 2 * big), BF16),
            pltpu.VMEM((128, 2 * big), BF16),
            pltpu.VMEM((1024, 128), BF16),
            pltpu.VMEM((1024, 128), BF16),
            pltpu.VMEM((NY, NZ, 128, 128), F32),
            pltpu.VMEM((NY, PAR, 128), F32),
            pltpu.VMEM((NY, 16, 128), F32),
        ]
        + ring_buffers((3, 64, 128), (3, ROWS - 64, 128))
        + ring_buffers((2, 64, 128), (2, ROWS - 64, 128))
        + ring_buffers((2, nb, COVER, 128), (2, nb, COVER, 128))
        + ring_buffers((2, COVER, 128), (1, COVER, 128))
        + ring_buffers((2, COVER, 128), (1, COVER, 128))
        + ring_buffers((1, COVER, 128), (1, COVER, 128))
        + [
            pltpu.VMEM((ZA, ROWS, 128), F32),
            pltpu.VMEM((NY, nb, COVER, 128), F32),
            pltpu.VMEM((NZ, COVER, 128), F32),
            pltpu.VMEM((NZ, COVER, 128), F32),
            pltpu.VMEM((NY, 16, 128), F32),
            pltpu.VMEM((NX, 16, 128), F32),
            pltpu.VMEM((NZ, 16, 128), F32),
            pltpu.VMEM((16, 128), F32),
            pltpu.VMEM((16, 128), F32),
            pltpu.SemaphoreType.DMA((19,)),
            pltpu.SemaphoreType.DMA((19,)),
            pltpu.SemaphoreType.DMA((9,)),
        ]
        + [pltpu.SemaphoreType.DMA((6,))] * 12
        + [
            pltpu.SemaphoreType.DMA((NZ,)),
            pltpu.SemaphoreType.DMA((NZ,)),
            pltpu.SemaphoreType.DMA((13,)),
            pltpu.SemaphoreType.DMA((13,)),
        ]
    )
    block, sums = pl.pallas_call(
        main_kernel,
        name="network",
        out_shape=[shape((COVER, 128), F32), shape((16, 128), F32)],
        in_specs=[ANY] * 7,
        out_specs=[VMEM, VMEM],
        scratch_shapes=scratch,
        compiler_params=pltpu.CompilerParams(
            collective_id=0, has_side_effects=True, vmem_limit_bytes=60 * 1024 * 1024
        ),
    )(track, orbit, *stations)

    owned, right, blocks = pl.pallas_call(
        finish_kernel,
        name="finish",
        out_shape=[
            shape((30, ROWS), F32),
            shape((1, ROWS), F32),
            shape((PAR, PAR, OWN), F32),
        ],
        in_specs=[VMEM, VMEM],
        out_specs=[VMEM] * 3,
    )(block, sums)
    return owned.T, right.reshape(ROWS), jnp.transpose(blocks, (2, 0, 1))


def solution(mesh):
    placed = (
        P(("sta", "sat"), None, None, None),
        P(("sta", "sat"), None, None),
        P(("sta", "sat"), None, None),
        P(("sta", "sat"), None, None),
        P(("sta", "sat"), None),
        P(("sta", "sat"), None),
        P("sat", None, None, None),
    )
    return jax.shard_map(
        shards,
        mesh=mesh,
        in_specs=placed,
        out_specs=(P("sat", "sta"), P("sat"), P("sat", None, None)),
        check_vma=False,
    )
```

time: 64 us -> 56.2 us (0.88)
  Pallas kernels: 59.2 us -> 54.9 us
  local copies, waits for them, and re-layouts: 2.22 us -> 0 us
  other arithmetic: 0.69 us -> 0 us
    pallas_call x1, Pallas kernels: 57.8 us -> 53.3 us  [shards(): pl.pallas_call(main_kernel, name='network', out_shape=[shape((COVER, 128)...]
    unnamed x3 -> x0, local copies, waits for them, and re-layouts: 2.22 us -> none
where the time goes in v3:
time: 56.2 us; the launch traced here: 55.5 us
  Pallas kernels  54.9 us (98%)
  between operations  0.64 us (1%)
    pallas_call x1, Pallas kernels, shards(): pl.pallas_call(main_kernel, name='network', out_shape=[shape((COVER, 128)...  53.3 us
    pallas_call x1, Pallas kernels, shards(): pl.pallas_call(finish_kernel, name='finish', out_shape=[shape((30, ROWS),...  1.59 us

profile of v3, /device:TPU:2, one launch (start us, length us, event | category | flops | bytes accessed | tf_op | source)
XLA Modules:
  0.0 55.5 jit_solution(13575890328493606048)
XLA Ops:
  0.6 53.3 %network.1 = (f32[40,128]{1,0:T(8,128)}, f32[16,128]{1,0:T(8,128)}) custom-call(s32[2,32]{1,0:T(2,128)} %refs_0_.1, f32[15,3,8,256]{3,2,1,0:T(8,128)} %refs_1_.1, f32[2,3,32,256]{3,2,1,0:T(8,128)} %refs_2_.1, f32[2,32,256]{2,1,0:T(8,128)} %refs_3_.1, f32[2,32,256]{2,1,0:T(8,128)} %refs_4_.1, s32[2,32,256]{2,1,0:T(8,128)} %refs_5_.1, s32[2,256]{1,0:T(2,128)} %refs_6_.1), custom_call_target="tpu_custom_call" | custom-call | tf_op jit(solution)/shard_map/network/pallas_call | solution.py:564
  53.9 1.6 %finish.1 = (f32[30,120]{1,0:T(8,128)}, f32[1,120]{1,0:T(1,128)}, f32[8,8,15]{2,1,0:T(8,128)}) custom-call(f32[40,128]{1,0:T(8,128)} %get-tuple-element.8.block, f32[16,128]{1,0:T(8,128)} %get-tuple-element.9.sums), custom_call_target="tpu_custom_call" | custom-call | tf_op jit(solution)/shard_map/finish/pallas_call | solution.py:576

commit v4 on v3

--- a/solution.py
+++ b/solution.py
@@ -24,7 +24,7 @@
 NX = 4
 NZ = 8
 ROWS = 120
-COVER = 40
+COVER = 32
 CUT = 8
 ZA = 5
 ANY = pl.BlockSpec(memory_space=pl.ANY)
@@ -202,14 +202,15 @@
     row8 = lax.broadcasted_iota(jnp.int32, (8, EPOCHS), 0)
     pick_last = jnp.where((lane_rows % 32 == 16) & (lane_rows < 96), 1.0, 0.0).astype(BF16)
 
+    pick[:, 4 * EPOCHS :] = pick_last
+
     def prepare(index):
         sight, mapping, residual, counts, knots = mine if index < 2 else other
         s = index % 2
         chosen = lane_rows % 32 == knots[s : s + 1, :] + KNOTS * index
         chosen = jnp.where(chosen & (lane_rows < 96), 1.0, 0.0)
-        wide = 2 * EPOCHS * index
+        wide = EPOCHS * index
         pick[:, wide : wide + EPOCHS] = chosen.astype(BF16)
-        pick[:, wide + EPOCHS : wide + 2 * EPOCHS] = pick_last
         weight = counts[s].astype(F32)
         path = mapping[s]
         seen = residual[s]
@@ -264,22 +265,24 @@
         def fill(k, second):
             row = pl.multiple_of(top + k * 16, 16)
             inner = pl.multiple_of(k * 16, 16)
+
+            def put(high_ref, low_ref, rows, lanes, value):
+                high_ref[pl.ds(rows, 16), lanes], low_ref[pl.ds(rows, 16), lanes] = halves(value)
+
+            gathered = 0.0
             for index in range(4):
                 lanes = slice(index * EPOCHS, (index + 1) * EPOCHS)
                 a = one(2 * k, index)
                 b = one(2 * k + 1, index) if second else [jnp.zeros_like(i) for i in a]
-                pieces = [halves(jnp.concatenate([i, j], axis=0)) for i, j in zip(a, b)]
+                values = [jnp.concatenate([i, j], axis=0) for i, j in zip(a, b)]
+                if diagonal:
+                    put(u_high, u_low, inner, lanes, values[1])
                 if sides:
-                    f_high[pl.ds(row, 16), lanes], f_low[pl.ds(row, 16), lanes] = pieces[0]
-                if diagonal:
-                    u_high[pl.ds(inner, 16), lanes], u_low[pl.ds(inner, 16), lanes] = pieces[1]
-                if sides:
-                    wide = 2 * EPOCHS * index
-                    for i in range(2):
-                        lanes = slice(wide + i * EPOCHS, wide + (i + 1) * EPOCHS)
-                        high, low = pieces[i - 2]
-                        t_high[pl.ds(inner, 16), lanes] = high
-                        t_low[pl.ds(inner, 16), lanes] = low
+                    put(f_high, f_low, row, lanes, values[0])
+                    put(t_high, t_low, inner, lanes, values[-2])
+                    gathered = gathered + values[-1]
+            if sides:
+                put(t_high, t_low, inner, slice(4 * EPOCHS, 5 * EPOCHS), gathered)
 
         def step(k, carry):
             fill(k, True)
@@ -297,7 +300,13 @@
             high, low = high.astype(F32), low.astype(F32)
             e_right[rows] = jnp.where((lane >= 32) & (lane < 64), low, high).astype(BF16)
         if diagonal:
-            own_sum[chip] = squeeze(product(u_high[...], u_low[...], u_high[...], u_low[...]))
+            rows = pl.ds(pl.multiple_of(top, 128), 128)
+            v_high, v_low = f_high[rows], f_low[rows]
+            own_sum[chip] = squeeze(
+                product(u_high[...], u_low[...], u_high[...], u_low[...])
+                - product(v_high, v_low, v_high, v_low)
+                - turned(e_left[rows], e_right[rows])
+            )
 
     for copy in keeps[1:]:
         copy.wait()
@@ -358,12 +367,17 @@
         result = product(f_high[rows], f_low[rows], r_high, r_low) + turned(e_left[rows], r_side)
         for i, slab in enumerate(slabs):
             lanes = slice(i * 128, (i + 1) * 128)
-            normal[slab, first : first + count] = -result[:, lanes].reshape(count, 128, 128)
+            for group in range(count):
+                for q in range(NX):
+                    at = group * 128 + q * 30
+                    normal[slab, first + group, q * COVER : (q + 1) * COVER] = -result[
+                        at : at + COVER, lanes
+                    ]
 
     def rows_of(peer):
-        return pl.ds(pl.multiple_of(jnp.minimum(peer * 30 // 8, 10) * 8, 8), COVER)
-
-    row_cut = (pl.ds(0, 64), pl.ds(64, ROWS - 64))
+        return pl.ds(pl.multiple_of(peer * COVER, COVER), COVER)
+
+    row_cut = (pl.ds(0, 64), pl.ds(64, 64))
     cuts = ((pl.ds(0, 2), pl.ds(2, 1)), (pl.ds(3, 1), pl.ds(4, 1)))
     b_cut = (pl.ds(0, 2), pl.ds(2, 1))
 
@@ -415,11 +429,11 @@
     a_1, a_2 = first_view(0), first_view(1)
     multiply(0, 3, (far, right))
     ay_1 = ring_start(a_1, y, bufs[0], sems[0], at_y, (0, 1, 2))
-    multiply(3, 2, (far, right))
-    ay_2 = ring_start(a_2, y, bufs[1], sems[1], at_y, (0, 1, 2))
     multiply(ZA, NZ - ZA, (far, right))
     multiply(ZA, NZ - ZA, (left, y))
     bx = ring_start(bx_view, x, bufs[2], sems[2], at_x, (0, 1, 2, 3))
+    multiply(3, 2, (far, right))
+    ay_2 = ring_start(a_2, y, bufs[1], sems[1], at_y, (0, 1, 2))
     multiply(0, 3, (left, y))
     ay_1 += ring_start(a_1, y, bufs[0], sems[0], at_y, (3,))
     multiply(3, 2, (left, y))
@@ -428,12 +442,12 @@
 
     build(far, c, False, True)
     for slab in range(NY):
-        small[slab, 0:8] = own_sum[slab] + squeeze(normal[slab, slab * 2 + c])
+        small[slab, 0:8] = own_sum[slab]
         small[slab, 8:16] = normal[slab, 0, ROWS : ROWS + 8, :]
     sy = small_start(0, lambda peer: small.at[peer], small_y, y, NY, at_y)
 
+    bx = ring_middle(bx_view, x, bufs[2], sems[2], at_x, bx)
     ay_2 = ring_middle(a_2, y, bufs[1], sems[1], at_y, ay_2)
-    bx = ring_middle(bx_view, x, bufs[2], sems[2], at_x, bx)
 
     c_1, c_2 = second_view(0), second_view(1)
     ring_finish(
@@ -481,14 +495,13 @@
 
 def finish_kernel(block, sums, owned, right, blocks):
     z, x, y, c = place()
-    skip = x * 30 - jnp.minimum(x * 30 // 8, 10) * 8
     cross_factor = SATS / math.sqrt(512 * EPOCHS)
     factor = SATS / (512 * SLOTS * EPOCHS)
-    value = pltpu.roll(block[...], COVER - skip, 0)[0:30, 0:ROWS]
+    value = block[0:30, 0:ROWS]
     row = (z * NX + x) * 30 + lax.broadcasted_iota(jnp.int32, (30, ROWS), 0)
     column = (y * 2 + c) * ROWS + lax.broadcasted_iota(jnp.int32, (30, ROWS), 1)
     owned[...] = jnp.where(row // PAR == column // PAR, 0.0, value) * cross_factor
-    right[...] = sums[8:9, 0:ROWS] * factor
+    right[...] = sums[14:15, 0:ROWS] * factor
     scaled = jnp.broadcast_to((sums[0:8] * factor)[:, None, :], (PAR, PAR, 128))
     place_of = lax.broadcasted_iota(jnp.int32, (PAR, PAR, 128), 2) % PAR
     inner = lax.broadcasted_iota(jnp.int32, (PAR, PAR, 128), 1)
@@ -524,23 +537,23 @@
             pltpu.VMEM((1024, big), BF16),
             pltpu.VMEM((128, big), BF16),
             pltpu.VMEM((128, big), BF16),
-            pltpu.VMEM((128, 2 * big), BF16),
-            pltpu.VMEM((128, 2 * big), BF16),
-            pltpu.VMEM((128, 2 * big), BF16),
+            pltpu.VMEM((128, big + EPOCHS), BF16),
+            pltpu.VMEM((128, big + EPOCHS), BF16),
+            pltpu.VMEM((128, big + EPOCHS), BF16),
             pltpu.VMEM((1024, 128), BF16),
             pltpu.VMEM((1024, 128), BF16),
             pltpu.VMEM((NY, NZ, 128, 128), F32),
             pltpu.VMEM((NY, PAR, 128), F32),
             pltpu.VMEM((NY, 16, 128), F32),
         ]
-        + ring_buffers((3, 64, 128), (3, ROWS - 64, 128))
-        + ring_buffers((2, 64, 128), (2, ROWS - 64, 128))
+        + ring_buffers((3, 64, 128), (3, 64, 128))
+        + ring_buffers((2, 64, 128), (2, 64, 128))
         + ring_buffers((2, nb, COVER, 128), (2, nb, COVER, 128))
         + ring_buffers((2, COVER, 128), (1, COVER, 128))
         + ring_buffers((2, COVER, 128), (1, COVER, 128))
         + ring_buffers((1, COVER, 128), (1, COVER, 128))
         + [
-            pltpu.VMEM((ZA, ROWS, 128), F32),
+            pltpu.VMEM((ZA, 128, 128), F32),
             pltpu.VMEM((NY, nb, COVER, 128), F32),
             pltpu.VMEM((NZ, COVER, 128), F32),
             pltpu.VMEM((NZ, COVER, 128), F32),

time: 56.2 us -> 55.7 us (level)
  no operation moved by 1% of the time
where the time goes in v4:
time: 55.7 us; the launch traced here: 55 us
  Pallas kernels  54.4 us (98%)
  between operations  0.64 us (1%)
    pallas_call x1, Pallas kernels, shards(): pl.pallas_call(main_kernel, name='network', out_shape=[shape((COVER, 128)...  52.8 us
    pallas_call x1, Pallas kernels, shards(): pl.pallas_call(finish_kernel, name='finish', out_shape=[shape((30, ROWS),...  1.58 us

profile of v4, /device:TPU:2, one launch (start us, length us, event | category | flops | bytes accessed | tf_op | source)
XLA Modules:
  0.0 55.0 jit_solution(5395900608584585730)
XLA Ops:
  0.6 52.8 %network.1 = (f32[32,128]{1,0:T(8,128)}, f32[16,128]{1,0:T(8,128)}) custom-call(s32[2,32]{1,0:T(2,128)} %refs_0_.1, f32[15,3,8,256]{3,2,1,0:T(8,128)} %refs_1_.1, f32[2,3,32,256]{3,2,1,0:T(8,128)} %refs_2_.1, f32[2,32,256]{2,1,0:T(8,128)} %refs_3_.1, f32[2,32,256]{2,1,0:T(8,128)} %refs_4_.1, s32[2,32,256]{2,1,0:T(8,128)} %refs_5_.1, s32[2,256]{1,0:T(2,128)} %refs_6_.1), custom_call_target="tpu_custom_call" | custom-call | tf_op jit(solution)/shard_map/network/pallas_call | solution.py:577
  53.5 1.6 %finish.1 = (f32[30,120]{1,0:T(8,128)}, f32[1,120]{1,0:T(1,128)}, f32[8,8,15]{2,1,0:T(8,128)}) custom-call(f32[32,128]{1,0:T(8,128)} %get-tuple-element.8.block, f32[16,128]{1,0:T(8,128)} %get-tuple-element.9.sums), custom_call_target="tpu_custom_call" | custom-call | tf_op jit(solution)/shard_map/finish/pallas_call | solution.py:589

commit v5 on v4

--- a/solution.py
+++ b/solution.py
@@ -26,7 +26,7 @@
 ROWS = 120
 COVER = 32
 CUT = 8
-ZA = 5
+ZA = 4
 ANY = pl.BlockSpec(memory_space=pl.ANY)
 VMEM = pl.BlockSpec(memory_space=pltpu.VMEM)
 SMEM = pl.BlockSpec(memory_space=pltpu.SMEM)
@@ -122,13 +122,13 @@
     mine, other, refs = refs[:5], refs[5:10], refs[10:]
     (track_s, ids_v, ids_w, ids_a, ids_b, full, sv, factors, f_high, f_low, u_high, u_low,
      t_high, t_low, pick, e_left, e_right, normal, own_sum, small), refs = refs[:20], refs[20:]
-    bufs, refs = [refs[i * 8 : (i + 1) * 8] for i in range(6)], refs[48:]
+    bufs, refs = [refs[i * 8 : (i + 1) * 8] for i in range(8)], refs[64:]
     (y_part, x_part, total, arrived, small_y, small_x, small_z, hold_x, hold_z), refs = (
         refs[:9], refs[9:])
     g_send, g_recv, local = refs[:3]
     refs = refs[3:]
-    sems = [(refs[2 * i], refs[2 * i + 1]) for i in range(6)]
-    z_send, z_recv, s_send, s_recv = refs[12:]
+    sems = [(refs[2 * i], refs[2 * i + 1]) for i in range(8)]
+    z_send, z_recv, s_send, s_recv = refs[16:]
     z, x, y, c = place()
 
     def at_y(peer):
@@ -378,21 +378,18 @@
         return pl.ds(pl.multiple_of(peer * COVER, COVER), COVER)
 
     row_cut = (pl.ds(0, 64), pl.ds(64, 64))
-    cuts = ((pl.ds(0, 2), pl.ds(2, 1)), (pl.ds(3, 1), pl.ds(4, 1)))
-    b_cut = (pl.ds(0, 2), pl.ds(2, 1))
-
-    def first_view(which):
-        zs = (pl.ds(0, 3), pl.ds(3, 2))[which]
-        return lambda peer, half: normal.at[peer, zs, row_cut[half]]
-
-    def second_view(which):
-        return lambda peer, half: y_part.at[cuts[which][half], rows_of(peer)]
-
-    def bx_view(peer, half):
-        return normal.at[pl.ds(2 * half, 2), pl.ds(ZA, NZ - ZA), rows_of(peer)]
-
-    def by_view(peer, half):
-        return x_part.at[peer, b_cut[half]]
+
+    def y_first(z0):
+        return lambda peer, half: normal.at[peer, pl.ds(z0, 2), row_cut[half]]
+
+    def y_then_x(z0):
+        return lambda peer, half: y_part.at[pl.ds(z0 + half, 1), rows_of(peer)]
+
+    def x_first(z0):
+        return lambda peer, half: normal.at[pl.ds(2 * half, 2), pl.ds(z0, 2), rows_of(peer)]
+
+    def x_then_y(z0):
+        return lambda peer, half: x_part.at[peer, pl.ds(z0 - ZA + half, 1)]
 
     def small_start(base, source, target, me, size, device):
         copies = []
@@ -426,19 +423,65 @@
             def _():
                 last_copy(peer, z).start()
 
-    a_1, a_2 = first_view(0), first_view(1)
-    multiply(0, 3, (far, right))
-    ay_1 = ring_start(a_1, y, bufs[0], sems[0], at_y, (0, 1, 2))
-    multiply(ZA, NZ - ZA, (far, right))
-    multiply(ZA, NZ - ZA, (left, y))
-    bx = ring_start(bx_view, x, bufs[2], sems[2], at_x, (0, 1, 2, 3))
-    multiply(3, 2, (far, right))
-    ay_2 = ring_start(a_2, y, bufs[1], sems[1], at_y, (0, 1, 2))
-    multiply(0, 3, (left, y))
-    ay_1 += ring_start(a_1, y, bufs[0], sems[0], at_y, (3,))
-    multiply(3, 2, (left, y))
-    ay_2 += ring_start(a_2, y, bufs[1], sems[1], at_y, (3,))
-    ay_1 = ring_middle(a_1, y, bufs[0], sems[0], at_y, ay_1)
+    class Ring:
+        def __init__(self, number, view, me, device):
+            self.number, self.view, self.me, self.device = number, view, me, device
+            self.copies = []
+
+        def start(self, slots=(0, 1, 2, 3)):
+            self.copies += ring_start(
+                self.view, self.me, bufs[self.number], sems[self.number], self.device, slots
+            )
+
+        def middle(self):
+            self.copies = ring_middle(
+                self.view, self.me, bufs[self.number], sems[self.number], self.device, self.copies
+            )
+
+        def finish(self, out_0, out_1):
+            ring_finish(self.view, self.me, bufs[self.number], self.copies, out_0, out_1)
+
+    firsts = [
+        Ring(0, y_first(0), y, at_y),
+        Ring(1, y_first(2), y, at_y),
+        Ring(2, x_first(4), x, at_x),
+        Ring(3, x_first(6), x, at_x),
+    ]
+    seconds = [
+        Ring(4, y_then_x(0), x, at_x),
+        Ring(5, y_then_x(2), x, at_x),
+        Ring(6, x_then_y(4), y, at_y),
+        Ring(7, x_then_y(6), y, at_y),
+    ]
+
+    def turn(k):
+        z0 = 2 * k
+        if z0 < ZA:
+            parts = [y_part.at[pl.ds(z0, 2), row_cut[half]] for half in range(2)]
+        else:
+            parts = [x_part.at[pl.ds(2 * half, 2), pl.ds(z0 - ZA, 2)] for half in range(2)]
+        firsts[k].finish(*parts)
+        seconds[k].start()
+
+    def close(k):
+        seconds[k].finish(total.at[pl.ds(2 * k, 1)], total.at[pl.ds(2 * k + 1, 1)])
+        send_last((2 * k, 2 * k + 1))
+
+    multiply(0, 2, (far, right))
+    firsts[0].start((0, 1, 2))
+    multiply(4, 2, (far, right))
+    multiply(4, 2, (left, y))
+    firsts[2].start()
+    multiply(0, 2, (left, y))
+    firsts[0].start((3,))
+    multiply(2, 2, (far, right))
+    multiply(2, 2, (left, y))
+    multiply(6, 2, (far, right))
+    multiply(6, 2, (left, y))
+    firsts[0].middle()
+    firsts[1].start()
+    firsts[2].middle()
+    firsts[3].start()
 
     build(far, c, False, True)
     for slab in range(NY):
@@ -446,37 +489,24 @@
         small[slab, 8:16] = normal[slab, 0, ROWS : ROWS + 8, :]
     sy = small_start(0, lambda peer: small.at[peer], small_y, y, NY, at_y)
 
-    bx = ring_middle(bx_view, x, bufs[2], sems[2], at_x, bx)
-    ay_2 = ring_middle(a_2, y, bufs[1], sems[1], at_y, ay_2)
-
-    c_1, c_2 = second_view(0), second_view(1)
-    ring_finish(
-        a_1, y, bufs[0], ay_1, y_part.at[pl.ds(0, 3), row_cut[0]], y_part.at[pl.ds(0, 3), row_cut[1]]
-    )
-    ax_1 = ring_start(c_1, x, bufs[3], sems[3], at_x, (0, 1, 2, 3))
-
+    turn(0)
+    turn(2)
+    firsts[1].middle()
+    firsts[3].middle()
     hold_x[...] = small_sum(sy, small_y, y, small[y], NY)
     sx = small_start(3, lambda peer: hold_x, small_x, x, NX, at_x)
-
-    ring_finish(bx_view, x, bufs[2], bx, x_part.at[pl.ds(0, 2)], x_part.at[pl.ds(2, 2)])
-    by = ring_start(by_view, y, bufs[4], sems[4], at_y, (0, 1, 2, 3))
-    ax_1 = ring_middle(c_1, x, bufs[3], sems[3], at_x, ax_1)
-    ring_finish(
-        a_2, y, bufs[1], ay_2, y_part.at[pl.ds(3, 2), row_cut[0]], y_part.at[pl.ds(3, 2), row_cut[1]]
-    )
-    ax_2 = ring_start(c_2, x, bufs[5], sems[5], at_x, (0, 1, 2, 3))
-
+    seconds[0].middle()
+    seconds[2].middle()
+    turn(1)
+    turn(3)
+    close(0)
+    close(2)
     hold_z[...] = small_sum(sx, small_x, x, hold_x[...], NX)
     sz = small_start(6, lambda peer: hold_z, small_z, z, NZ, at_z)
-
-    by = ring_middle(by_view, y, bufs[4], sems[4], at_y, by)
-    ax_2 = ring_middle(c_2, x, bufs[5], sems[5], at_x, ax_2)
-    ring_finish(c_1, x, bufs[3], ax_1, total.at[pl.ds(0, 2)], total.at[pl.ds(2, 1)])
-    send_last((0, 1, 2))
-    ring_finish(by_view, y, bufs[4], by, total.at[pl.ds(ZA, 2)], total.at[pl.ds(ZA + 2, 1)])
-    send_last((5, 6, 7))
-    ring_finish(c_2, x, bufs[5], ax_2, total.at[pl.ds(3, 1)], total.at[pl.ds(4, 1)])
-    send_last((3, 4))
+    seconds[1].middle()
+    seconds[3].middle()
+    close(1)
+    close(3)
 
     out_small[...] = small_sum(sz, small_z, z, hold_z[...], NZ)
     value = total[z]
@@ -486,7 +516,7 @@
         value = value + arrived[peer]
     out[...] = value
     sent = [right_head, left_tail, right_tail, left_head, relay_right, relay_left]
-    for copies in (sent, swaps, mates, sy, sx, sz, ay_1, ay_2, bx, ax_1, by, ax_2):
+    for copies in [sent, swaps, mates, sy, sx, sz] + [ring.copies for ring in firsts + seconds]:
         for copy in copies:
             copy.wait_send()
     for k in range(1, NZ):
@@ -546,12 +576,9 @@
             pltpu.VMEM((NY, PAR, 128), F32),
             pltpu.VMEM((NY, 16, 128), F32),
         ]
-        + ring_buffers((3, 64, 128), (3, 64, 128))
-        + ring_buffers((2, 64, 128), (2, 64, 128))
-        + ring_buffers((2, nb, COVER, 128), (2, nb, COVER, 128))
-        + ring_buffers((2, COVER, 128), (1, COVER, 128))
-        + ring_buffers((2, COVER, 128), (1, COVER, 128))
-        + ring_buffers((1, COVER, 128), (1, COVER, 128))
+        + ring_buffers((2, 64, 128), (2, 64, 128)) * 2
+        + ring_buffers((2, 2, COVER, 128), (2, 2, COVER, 128)) * 2
+        + ring_buffers((1, COVER, 128), (1, COVER, 128)) * 4
         + [
             pltpu.VMEM((ZA, 128, 128), F32),
             pltpu.VMEM((NY, nb, COVER, 128), F32),
@@ -566,7 +593,7 @@
             pltpu.SemaphoreType.DMA((19,)),
             pltpu.SemaphoreType.DMA((9,)),
         ]
-        + [pltpu.SemaphoreType.DMA((6,))] * 12
+        + [pltpu.SemaphoreType.DMA((6,))] * 16
         + [
             pltpu.SemaphoreType.DMA((NZ,)),
             pltpu.SemaphoreType.DMA((NZ,)),

time: 55.7 us -> 54.4 us (0.977)
  Pallas kernels: 54.4 us -> 53 us
    pallas_call x1, Pallas kernels: 52.8 us -> 51.5 us  [shards(): pl.pallas_call(main_kernel, name='network', out_shape=[shape((COVER, 128)...]
where the time goes in v5:
time: 54.4 us; the launch traced here: 53.7 us
  Pallas kernels  53 us (97%)
  between operations  0.64 us (1%)
    pallas_call x1, Pallas kernels, shards(): pl.pallas_call(main_kernel, name='network', out_shape=[shape((COVER, 128)...  51.5 us
    pallas_call x1, Pallas kernels, shards(): pl.pallas_call(finish_kernel, name='finish', out_shape=[shape((30, ROWS),...  1.58 us

profile of v5, /device:TPU:2, one launch (start us, length us, event | category | flops | bytes accessed | tf_op | source)
XLA Modules:
  0.0 53.7 jit_solution(17714020192046927626)
XLA Ops:
  0.6 51.5 %network.1 = (f32[32,128]{1,0:T(8,128)}, f32[16,128]{1,0:T(8,128)}) custom-call(s32[2,32]{1,0:T(2,128)} %refs_0_.1, f32[15,3,8,256]{3,2,1,0:T(8,128)} %refs_1_.1, f32[2,3,32,256]{3,2,1,0:T(8,128)} %refs_2_.1, f32[2,32,256]{2,1,0:T(8,128)} %refs_3_.1, f32[2,32,256]{2,1,0:T(8,128)} %refs_4_.1, s32[2,32,256]{2,1,0:T(8,128)} %refs_5_.1, s32[2,256]{1,0:T(2,128)} %refs_6_.1), custom_call_target="tpu_custom_call" | custom-call | tf_op jit(solution)/shard_map/network/pallas_call | solution.py:604
  52.1 1.6 %finish.1 = (f32[30,120]{1,0:T(8,128)}, f32[1,120]{1,0:T(1,128)}, f32[8,8,15]{2,1,0:T(8,128)}) custom-call(f32[32,128]{1,0:T(8,128)} %get-tuple-element.8.block, f32[16,128]{1,0:T(8,128)} %get-tuple-element.9.sums), custom_call_target="tpu_custom_call" | custom-call | tf_op jit(solution)/shard_map/finish/pallas_call | solution.py:616

commit v6 on v5

--- a/solution.py
+++ b/solution.py
@@ -25,7 +25,9 @@
 NZ = 8
 ROWS = 120
 COVER = 32
-CUT = 8
+HEAD = (0, 5)
+TAIL = (5, 4)
+REST = (9, 6)
 ZA = 4
 ANY = pl.BlockSpec(memory_space=pl.ANY)
 VMEM = pl.BlockSpec(memory_space=pltpu.VMEM)
@@ -142,7 +144,8 @@
 
     mate = (z * NX + x, y * 2 + 1 - c)
     far, right, left = (y + 2) % NY, (y + 1) % NY, (y + 3) % NY
-    head, tail = (0, CUT), (CUT, OWN - CUT)
+    twin = at_x(x + 1 - 2 * (x % 2))
+    share, share_twin = (REST[0] + 3 * (x % 2), 3), (REST[0] + 3 - 3 * (x % 2), 3)
 
     def base_of(chip, core):
         return (chip * 2 + core) * OWN
@@ -172,17 +175,24 @@
         + [mate]
     )
 
-    def go(slot, src, dst, device):
+    everything = []
+
+    def go(src, dst, device):
+        slot = len(everything)
         copy = remote(src, dst, g_send.at[slot], g_recv.at[slot], device)
         copy.start()
+        everything.append(copy)
         return copy
 
-    right_head = go(0, own(head), part(y, head), at_y(right))
-    left_tail = go(1, own(tail), part(y, tail), at_y(left))
-    right_tail = go(2, own(tail), part(y, tail), at_y(right))
-    left_head = go(3, own(head), part(y, head), at_y(left))
-    swaps = [go(7 + i, a, b, mate) for i, (a, b) in enumerate(zip(given, other))]
-    mate_own = go(12, orbit, full.at[pl.ds(base_of(y, c), OWN)], mate)
+    def pass_on(chip, cut, device):
+        return go(part(chip, cut), part(chip, cut), device)
+
+    share_right = go(own(share), part(y, share), at_y(right))
+    share_left = go(own(share), part(y, share), at_y(left))
+    head_right = go(own(HEAD), part(y, HEAD), at_y(right))
+    tail_left = go(own(TAIL), part(y, TAIL), at_y(left))
+    swaps = [go(a, b, mate) for a, b in zip(given, other)]
+    mate_own = go(orbit, full.at[pl.ds(base_of(y, c), OWN)], mate)
 
     keeps[0].wait()
     place_lane = lax.broadcasted_iota(jnp.int32, (1, 128), 1)
@@ -193,7 +203,7 @@
         ids_v[s : s + 1, :] = slots
     hand_a = pltpu.make_async_copy(ids_v, ids_a, local.at[7])
     hand_a.start()
-    swaps.append(go(6, ids_v, ids_w, mate))
+    swaps.append(go(ids_v, ids_w, mate))
 
     blank = jnp.zeros((4, 3, 8, EPOCHS), F32)
     sv[:, :, SLOTS:, :] = blank
@@ -321,32 +331,53 @@
     right_scale = jnp.where(lane % 32 < 16, scale, 1.0)
     special = jnp.where(lane % 32 == 16, -1.0, local_rows[1:2] * scale)
     hand_b.wait()
+    first, second = (share[0], 2), (share[0] + 2, 1)
+    share_right.wait_recv()
+    far_first = pass_on(left, first, at_y(right))
+    twin_left = pass_on(left, share, twin)
+    share_left.wait_recv()
+    far_second = pass_on(right, second, at_y(left))
+    twin_right = pass_on(right, share, twin)
+    tail_right = go(own(TAIL), part(y, TAIL), at_y(right))
+    head_left = go(own(HEAD), part(y, HEAD), at_y(left))
     build(y, c, True, True)
-    mates = [mate_own]
-    right_head.wait_recv()
-    relay_right = go(4, part(left, head), part(left, head), at_y(right))
-    mates.append(go(13, part(left, head), part(left, head), mate))
-    left_tail.wait_recv()
-    relay_left = go(5, part(right, tail), part(right, tail), at_y(left))
-    mates.append(go(14, part(right, tail), part(right, tail), mate))
+
+    head_right.wait_recv()
+    far_head = pass_on(left, HEAD, at_y(right))
+    mates_left = [pass_on(left, HEAD, mate)]
+    tail_left.wait_recv()
+    far_tail = pass_on(right, TAIL, at_y(left))
+    mates_right = [pass_on(right, TAIL, mate)]
+    far_first.wait_recv()
+    far_second.wait_recv()
+    twin_far = pass_on(far, share, twin)
+    mates_far = [pass_on(far, share, mate)]
+    twin_left.wait_recv()
+    mates_left.append(pass_on(left, REST, mate))
+    twin_right.wait_recv()
+    mates_right.append(pass_on(right, REST, mate))
     mate_own.wait_recv()
     build(y, 1 - c, True, False)
-    right_tail.wait_recv()
-    mates.append(go(15, part(left, tail), part(left, tail), mate))
-    left_head.wait_recv()
-    mates.append(go(16, part(right, head), part(right, head), mate))
+    tail_right.wait_recv()
+    mates_left.append(pass_on(left, TAIL, mate))
+    head_left.wait_recv()
+    mates_right.append(pass_on(right, HEAD, mate))
     build(left, c, True, True)
+    twin_far.wait_recv()
+    mates_far.append(pass_on(far, share_twin, mate))
     build(right, c, True, True)
-    for copy in mates[1:]:
+    far_head.wait_recv()
+    mates_far.append(pass_on(far, HEAD, mate))
+    far_tail.wait_recv()
+    mates_far.append(pass_on(far, TAIL, mate))
+    for copy in mates_left:
         copy.wait_recv()
     build(left, 1 - c, True, False)
+    for copy in mates_right:
+        copy.wait_recv()
     build(right, 1 - c, True, False)
-    relay_right.wait_recv()
-    mates.append(go(17, part(far, head), part(far, head), mate))
-    relay_left.wait_recv()
-    mates.append(go(18, part(far, tail), part(far, tail), mate))
     build(far, c, True, False)
-    for copy in mates[5:]:
+    for copy in mates_far:
         copy.wait_recv()
     build(far, 1 - c, True, False)
 
@@ -515,8 +546,7 @@
         last_copy(peer, peer).wait_recv()
         value = value + arrived[peer]
     out[...] = value
-    sent = [right_head, left_tail, right_tail, left_head, relay_right, relay_left]
-    for copies in [sent, swaps, mates, sy, sx, sz] + [ring.copies for ring in firsts + seconds]:
+    for copies in [everything, sy, sx, sz] + [ring.copies for ring in firsts + seconds]:
         for copy in copies:
             copy.wait_send()
     for k in range(1, NZ):
@@ -589,8 +619,8 @@
             pltpu.VMEM((NZ, 16, 128), F32),
             pltpu.VMEM((16, 128), F32),
             pltpu.VMEM((16, 128), F32),
-            pltpu.SemaphoreType.DMA((19,)),
-            pltpu.SemaphoreType.DMA((19,)),
+            pltpu.SemaphoreType.DMA((30,)),
+            pltpu.SemaphoreType.DMA((30,)),
             pltpu.SemaphoreType.DMA((9,)),
         ]
         + [pltpu.SemaphoreType.DMA((6,))] * 16

time: 54.4 us -> 53.8 us (0.989)
  Pallas kernels: 53 us -> 52.2 us
    pallas_call x1, Pallas kernels: 51.5 us -> 50.7 us  [shards(): pl.pallas_call(main_kernel, name='network', out_shape=[shape((COVER, 128)...]
where the time goes in v6:
time: 53.8 us; the launch traced here: 52.9 us
  Pallas kernels  52.2 us (97%)
  between operations  0.64 us (1%)
    pallas_call x1, Pallas kernels, shards(): pl.pallas_call(main_kernel, name='network', out_shape=[shape((COVER, 128)...  50.7 us
    pallas_call x1, Pallas kernels, shards(): pl.pallas_call(finish_kernel, name='finish', out_shape=[shape((30, ROWS),...  1.58 us

profile of v6, /device:TPU:2, one launch (start us, length us, event | category | flops | bytes accessed | tf_op | source)
XLA Modules:
  0.0 52.9 jit_solution(17106349684886179186)
XLA Ops:
  0.6 50.7 %network.1 = (f32[32,128]{1,0:T(8,128)}, f32[16,128]{1,0:T(8,128)}) custom-call(s32[2,32]{1,0:T(2,128)} %refs_0_.1, f32[15,3,8,256]{3,2,1,0:T(8,128)} %refs_1_.1, f32[2,3,32,256]{3,2,1,0:T(8,128)} %refs_2_.1, f32[2,32,256]{2,1,0:T(8,128)} %refs_3_.1, f32[2,32,256]{2,1,0:T(8,128)} %refs_4_.1, s32[2,32,256]{2,1,0:T(8,128)} %refs_5_.1, s32[2,256]{1,0:T(2,128)} %refs_6_.1), custom_call_target="tpu_custom_call" | custom-call | tf_op jit(solution)/shard_map/network/pallas_call | solution.py:634
  51.3 1.6 %finish.1 = (f32[30,120]{1,0:T(8,128)}, f32[1,120]{1,0:T(1,128)}, f32[8,8,15]{2,1,0:T(8,128)}) custom-call(f32[32,128]{1,0:T(8,128)} %get-tuple-element.8.block, f32[16,128]{1,0:T(8,128)} %get-tuple-element.9.sums), custom_call_target="tpu_custom_call" | custom-call | tf_op jit(solution)/shard_map/finish/pallas_call | solution.py:646

commit v7 on v6

--- a/solution.py
+++ b/solution.py
@@ -510,15 +510,15 @@
     multiply(6, 2, (far, right))
     multiply(6, 2, (left, y))
     firsts[0].middle()
-    firsts[1].start()
-    firsts[2].middle()
-    firsts[3].start()
-
     build(far, c, False, True)
     for slab in range(NY):
         small[slab, 0:8] = own_sum[slab]
         small[slab, 8:16] = normal[slab, 0, ROWS : ROWS + 8, :]
     sy = small_start(0, lambda peer: small.at[peer], small_y, y, NY, at_y)
+
+    firsts[1].start()
+    firsts[2].middle()
+    firsts[3].start()
 
     turn(0)
     turn(2)

time: 53.8 us -> 54 us (level)
  no operation moved by 1% of the time
where the time goes in v7:
time: 54 us; the launch traced here: 53.3 us
  Pallas kernels  52.6 us (97%)
  between operations  0.64 us (1%)
    pallas_call x1, Pallas kernels, shards(): pl.pallas_call(main_kernel, name='network', out_shape=[shape((COVER, 128)...  51 us
    pallas_call x1, Pallas kernels, shards(): pl.pallas_call(finish_kernel, name='finish', out_shape=[shape((30, ROWS),...  1.58 us

profile of v7, /device:TPU:2, one launch (start us, length us, event | category | flops | bytes accessed | tf_op | source)
XLA Modules:
  0.0 53.3 jit_solution(9375433630437432966)
XLA Ops:
  0.6 51.0 %network.1 = (f32[32,128]{1,0:T(8,128)}, f32[16,128]{1,0:T(8,128)}) custom-call(s32[2,32]{1,0:T(2,128)} %refs_0_.1, f32[15,3,8,256]{3,2,1,0:T(8,128)} %refs_1_.1, f32[2,3,32,256]{3,2,1,0:T(8,128)} %refs_2_.1, f32[2,32,256]{2,1,0:T(8,128)} %refs_3_.1, f32[2,32,256]{2,1,0:T(8,128)} %refs_4_.1, s32[2,32,256]{2,1,0:T(8,128)} %refs_5_.1, s32[2,256]{1,0:T(2,128)} %refs_6_.1), custom_call_target="tpu_custom_call" | custom-call | tf_op jit(solution)/shard_map/network/pallas_call | solution.py:634
  51.7 1.6 %finish.1 = (f32[30,120]{1,0:T(8,128)}, f32[1,120]{1,0:T(1,128)}, f32[8,8,15]{2,1,0:T(8,128)}) custom-call(f32[32,128]{1,0:T(8,128)} %get-tuple-element.8.block, f32[16,128]{1,0:T(8,128)} %get-tuple-element.9.sums), custom_call_target="tpu_custom_call" | custom-call | tf_op jit(solution)/shard_map/finish/pallas_call | solution.py:646
